TPU v7x, 32 devices: a whole 2x2x4 slice. The times are simulated.
32 devices in a mesh: dp: 16 (over z, y, x), tensor: 2 (over core).
Axes of the slice: x: 2, y: 2, z: 4, core: 2. Of those that a mesh axis runs over, the one named last changes fastest.
Arguments:
- latent_x: bfloat16 [1280, 16384], P('tensor', 'dp'), parts along dimension 1, may hold values from -6 to 6
- control_h: bfloat16 [1280, 16384], P('tensor', 'dp'), parts along dimension 1, may hold values from -6 to 6
- tile_mask: int32 [16, 8, 8], P('dp'), parts along dimension 0, may hold values 0 or 1
- timestep: int32 [16], P('dp'), parts along dimension 0, may hold values from 0 to 999
- time_weight: bfloat16 [320, 1280], P(None, 'tensor'), may hold values from -0.5 to 0.5
- norm_gain: float32 [3, 1280], P(None, 'tensor'), may hold values from 0.5 to 1.5
- norm_bias: float32 [3, 1280], P(None, 'tensor'), may hold values from -3 to 3
- unet_conv_in: bfloat16 [9, 1280, 1280], P(None, 'tensor'), may hold values from -0.0546875 to 0.0546875
- unet_conv_out: bfloat16 [9, 1280, 1280], P(None, 'tensor'), may hold values from -0.0546875 to 0.0546875
- control_conv: bfloat16 [9, 1280, 1280], P(None, 'tensor'), may hold values from -0.0546875 to 0.0546875
- unet_temb: bfloat16 [1280, 1280], P('tensor'), may hold values from -0.15625 to 0.15625
- control_temb: bfloat16 [1280, 1280], P('tensor'), may hold values from -0.15625 to 0.15625
- zero_conv: bfloat16 [1280, 1280], P('tensor'), may hold values from -0.15625 to 0.15625
Outputs:
- mixed: bfloat16 [1280, 16384], P('tensor', 'dp'), parts along dimension 1
There are 16 independent parts, one for each index of `dp`. A program takes and returns all parts, laid end to end along the dimension named above; an argument that names none is the same for every part. Nothing has to cross between parts.
All inputs are finite; a program needn't handle non-finite values.
Results may differ from a plain program's by a relative error of at most 0.014.
Values may be sent and summed in bfloat16 or wider, within the bound.
No kernel may reach another device: no remote copies, remote signals or barrier semaphores. Data moves between devices by JAX's collectives and lax.ppermute only.
A program may use at most 192 MiB of HBM per device.

v0:
```python
import math

import jax
import jax.numpy as jnp
from jax import lax
from jax.sharding import PartitionSpec as P

C = 1280
GROUPS = 32
FREQ = 320
S = 32
TILE = 4
VIEWS = 1


def timestep_features(timestep):
    half_width = FREQ // 2
    rates = jnp.exp(-math.log(10000.0) * jnp.arange(half_width, dtype=jnp.float32) / half_width)
    angles = timestep.astype(jnp.float32)[0] * rates
    return jnp.concatenate([jnp.cos(angles), jnp.sin(angles)])


def norm_silu(inputs, scales, shifts):
    rows_count = inputs.shape[0]
    group_size = C // GROUPS
    grouped = inputs.astype(jnp.float32).reshape(rows_count // group_size, group_size, VIEWS, S * S)
    average = jnp.mean(grouped, axis=(1, 3), keepdims=True)
    centred = grouped - average
    variance = jnp.mean(centred * centred, axis=(1, 3), keepdims=True)
    normed = (centred * lax.rsqrt(variance + 1e-05)).reshape(rows_count, VIEWS * S * S)
    return jax.nn.silu(normed * scales[:, None] + shifts[:, None]).astype(jnp.bfloat16)


def tap_mask(place, cells):
    where = jnp.arange(cells, dtype=jnp.int32)
    row_index = where // S % S + (place // 3 - 1)
    col_index = where % S + (place % 3 - 1)
    inside = (row_index >= 0) & (row_index < S) & (col_index >= 0) & (col_index < S)
    return inside.astype(jnp.float32)


def shift_cells(values, place):
    cells = values.shape[1]
    offset_cells = (place // 3 - 1) * S + (place % 3 - 1)
    padded = jnp.pad(values, ((0, 0), (S + 1, S + 1)))
    moved = lax.slice_in_dim(padded, S + 1 + offset_cells, S + 1 + offset_cells + cells, axis=1)
    return moved * tap_mask(place, cells)[None, :]


def conv_plain(weights, inputs, running):
    for place in range(9):
        product = jnp.dot(weights[place], inputs, preferred_element_type=jnp.float32)
        running = running + shift_cells(product, place)
    return running


def conv_flipped(weights, inputs):
    running = None
    for place in range(9):
        product = lax.dot_general(
            weights[place], inputs, (((0,), (0,)), ((), ())), preferred_element_type=jnp.float32
        )
        moved = shift_cells(product, place)
        running = moved if running is None else running + moved
    return running


def expand_mask(tile_mask):
    blocks = tile_mask.astype(jnp.float32)[:, :, None, :, None]
    spread_mask = jnp.broadcast_to(blocks, (VIEWS, S // TILE, TILE, S // TILE, TILE))
    return spread_mask.reshape(VIEWS * S * S)


def local(
    latent_x,
    control_h,
    tile_mask,
    timestep,
    time_weight,
    norm_gain,
    norm_bias,
    unet_conv_in,
    unet_conv_out,
    control_conv,
    unet_temb,
    control_temb,
    zero_conv,
):
    local_time = jax.nn.silu(
        jnp.dot(
            timestep_features(timestep),
            time_weight.astype(jnp.float32),
            precision=lax.Precision.HIGHEST,
        )
    )
    time_vector = lax.all_gather(local_time, "tensor", axis=0, tiled=True)
    unet_shift = jnp.dot(
        unet_temb.astype(jnp.float32), time_vector, precision=lax.Precision.HIGHEST
    )
    control_shift = jnp.dot(
        control_temb.astype(jnp.float32), time_vector, precision=lax.Precision.HIGHEST
    )
    gate_row = expand_mask(tile_mask)
    channels = latent_x.shape[0]
    first = norm_silu(latent_x, norm_gain[0], norm_bias[0])
    initial = jnp.zeros((channels, latent_x.shape[1]), jnp.float32)
    weights = unet_conv_in
    hidden_sum = conv_plain(weights, lax.all_gather(first, "tensor", axis=0, tiled=True), initial)
    hidden = (hidden_sum + unet_shift[:, None]).astype(jnp.bfloat16)
    hidden = lax.optimization_barrier(hidden)
    second = norm_silu(hidden, norm_gain[1], norm_bias[1])
    control_act = norm_silu(control_h, norm_gain[2], norm_bias[2])
    weights = control_conv
    control_sum = lax.psum_scatter(
        conv_flipped(weights, control_act).astype(jnp.bfloat16),
        "tensor",
        scatter_dimension=0,
        tiled=True,
    ).astype(jnp.float32)
    control_state = (control_h.astype(jnp.float32) + control_sum + control_shift[:, None]).astype(
        jnp.bfloat16
    )
    weights = zero_conv
    product = lax.dot_general(
        weights, control_state, (((0,), (0,)), ((), ())), preferred_element_type=jnp.float32
    )
    weights = unet_conv_out
    combined = lax.psum_scatter(
        (conv_flipped(weights, second) + product * gate_row[None, :]).astype(jnp.bfloat16),
        "tensor",
        scatter_dimension=0,
        tiled=True,
    ).astype(jnp.float32)
    return (latent_x.astype(jnp.float32) + combined).astype(jnp.bfloat16)


def solution(mesh):
    placed = (
        P("tensor", "dp"),
        P("tensor", "dp"),
        P("dp", None, None),
        P("dp"),
        P(None, "tensor"),
        P(None, "tensor"),
        P(None, "tensor"),
        P(None, "tensor", None),
        P(None, "tensor", None),
        P(None, "tensor", None),
        P("tensor", None),
        P("tensor", None),
        P("tensor", None),
    )
    return jax.shard_map(
        local, mesh=mesh, in_specs=placed, out_specs=P("tensor", "dp"), check_vma=False
    )
```

profile of v0, /device:TPU:0, one launch (start us, length us, event | category | flops | bytes accessed | tf_op | source)
XLA Modules:
  0.0 243.8 jit_solution(7723583734087239055)
XLA Ops:
  6.5 1.8 copy.23
  8.4 0.2 convert_reduce_fusion.1
  8.6 0.1 reduce_sum.70
  8.7 0.1 reduce_sum.74
  8.9 0.1 sub.162
  9.0 0.4 fusion.68
  9.5 0.1 reduce_sum.77
  9.7 0.1 mul.353
  9.9 2.0 fusion.76
  11.9 2.2 copy.24
  14.1 0.2 convert_reduce_fusion
  14.5 0.1 reduce_sum.110
  14.7 0.1 sub.171
  14.8 0.4 fusion.59
  15.2 0.1 reduce_sum.113
  15.4 0.1 mul.412
  15.6 6.7 %convolution_bitcast_fusion = f32[1280,1024]{0,1:T(8,128)} fusion(bf16[9,640,1280]{2,1,0:T(8,128)(2,1)} %param.22, bf16[640,1024]{0,1:T(8,128)(2,1)S(1)} %copy.24, f32[640]{0:T(1024)S(1)} %get-tuple-element.8, f32[640]{0:T(1024)S(1)} %get-tuple-element.13, f32[640]{0:T(1024)S(1)} %mul.412, f32[640]{0:T(1024)S(1)} %sub.171), kind=kOutput, calls=%fused_computation.51 | convolution fusion | flops 1684275200 | bytes 8202240 | tf_op jit(solution)/shard_map/dot_general | solution.py:60
  22.3 6.8 %convolution_bitcast_fusion.1 = f32[1280,1024]{0,1:T(8,128)} fusion(bf16[9,640,1280]{2,1,0:T(8,128)(2,1)} %param.22, bf16[640,1024]{0,1:T(8,128)(2,1)S(1)} %copy.24, f32[640]{0:T(1024)S(1)} %get-tuple-element.8, f32[640]{0:T(1024)S(1)} %get-tuple-element.13, f32[640]{0:T(1024)S(1)} %mul.412, f32[640]{0:T(1024)S(1)} %sub.171), kind=kOutput, calls=%fused_computation.52 | convolution fusion | flops 1684275200 | bytes 8202240 | tf_op jit(solution)/shard_map/dot_general | solution.py:60
  29.1 5.1 %convolution_bitcast_fusion.2 = f32[1280,1024]{0,1:T(8,128)} fusion(bf16[9,640,1280]{2,1,0:T(8,128)(2,1)S(1)} %bitcast.164, bf16[640,1024]{0,1:T(8,128)(2,1)S(1)} %copy.24, f32[640]{0:T(1024)S(1)} %get-tuple-element.8, f32[640]{0:T(1024)S(1)} %get-tuple-element.13, f32[640]{0:T(1024)S(1)} %mul.412, f32[640]{0:T(1024)S(1)} %sub.171), kind=kOutput, calls=%fused_computation.53 | convolution fusion | flops 1684275200 | bytes 8208384 | tf_op jit(solution)/shard_map/dot_general | solution.py:60
  34.2 5.1 %convolution_bitcast_fusion.3 = f32[1280,1024]{0,1:T(8,128)} fusion(bf16[9,640,1280]{2,1,0:T(8,128)(2,1)S(1)} %bitcast.164, bf16[640,1024]{0,1:T(8,128)(2,1)S(1)} %copy.24, f32[640]{0:T(1024)S(1)} %get-tuple-element.8, f32[640]{0:T(1024)S(1)} %get-tuple-element.13, f32[640]{0:T(1024)S(1)} %mul.412, f32[640]{0:T(1024)S(1)} %sub.171), kind=kOutput, calls=%fused_computation.54 | convolution fusion | flops 1684275200 | bytes 8208384 | tf_op jit(solution)/shard_map/dot_general | solution.py:60
  39.3 5.2 %convolution_bitcast_fusion.4 = f32[1280,1024]{0,1:T(8,128)} fusion(bf16[9,640,1280]{2,1,0:T(8,128)(2,1)S(1)} %bitcast.164, bf16[640,1024]{0,1:T(8,128)(2,1)S(1)} %copy.24, f32[640]{0:T(1024)S(1)} %get-tuple-element.8, f32[640]{0:T(1024)S(1)} %get-tuple-element.13, f32[640]{0:T(1024)S(1)} %mul.412, f32[640]{0:T(1024)S(1)} %sub.171), kind=kOutput, calls=%fused_computation.55 | convolution fusion | flops 1684275200 | bytes 8208384 | tf_op jit(solution)/shard_map/dot_general | solution.py:60
  44.4 5.1 %convolution_bitcast_fusion.5 = f32[1280,1024]{0,1:T(8,128)} fusion(bf16[9,640,1280]{2,1,0:T(8,128)(2,1)S(1)} %bitcast.164, bf16[640,1024]{0,1:T(8,128)(2,1)S(1)} %copy.24, f32[640]{0:T(1024)S(1)} %get-tuple-element.8, f32[640]{0:T(1024)S(1)} %get-tuple-element.13, f32[640]{0:T(1024)S(1)} %mul.412, f32[640]{0:T(1024)S(1)} %sub.171), kind=kOutput, calls=%fused_computation.56 | convolution fusion | flops 1684275200 | bytes 8208384 | tf_op jit(solution)/shard_map/dot_general | solution.py:60
  49.5 5.1 %convolution_bitcast_fusion.6 = f32[1280,1024]{0,1:T(8,128)} fusion(bf16[9,640,1280]{2,1,0:T(8,128)(2,1)S(1)} %bitcast.164, bf16[640,1024]{0,1:T(8,128)(2,1)S(1)} %copy.24, f32[640]{0:T(1024)S(1)} %get-tuple-element.8, f32[640]{0:T(1024)S(1)} %get-tuple-element.13, f32[640]{0:T(1024)S(1)} %mul.412, f32[640]{0:T(1024)S(1)} %sub.171), kind=kOutput, calls=%fused_computation.57 | convolution fusion | flops 1684275200 | bytes 8208384 | tf_op jit(solution)/shard_map/dot_general | solution.py:60
  54.6 5.0 %convolution_bitcast_fusion.7 = f32[1280,1024]{0,1:T(8,128)} fusion(bf16[9,640,1280]{2,1,0:T(8,128)(2,1)S(1)} %bitcast.164, bf16[640,1024]{0,1:T(8,128)(2,1)S(1)} %copy.24, f32[640]{0:T(1024)S(1)} %get-tuple-element.8, f32[640]{0:T(1024)S(1)} %get-tuple-element.13, f32[640]{0:T(1024)S(1)} %mul.412, f32[640]{0:T(1024)S(1)} %sub.171), kind=kOutput, calls=%fused_computation.58 | convolution fusion | flops 1684275200 | bytes 8208384 | tf_op jit(solution)/shard_map/dot_general | solution.py:60
  59.7 17.1 %fusion.27 = bf16[1280,1024]{0,1:T(8,128)(2,1)} fusion(f32[1280,1024]{0,1:T(8,128)} %convolution_bitcast_fusion.7, f32[1280,1024]{0,1:T(8,128)} %convolution_bitcast_fusion.6, f32[1280,1024]{0,1:T(8,128)} %convolution_bitcast_fusion.5, f32[1280,1024]{0,1:T(8,128)} %convolution_bitcast_fusion.4, f32[1280,1024]{0,1:T(8,128)} %convolution_bitcast_fusion.3, ...), kind=kOutput, calls=%fused_computation.43 | convolution fusion | flops 1707868160 | bytes 47560704 | tf_op jit(solution)/shard_map/dot_general | solution.py:60
  76.8 4.5 %copy.26 = bf16[1280,1024]{1,0:T(8,128)(2,1)} copy(bf16[1280,1024]{0,1:T(8,128)(2,1)} %fusion.27) | data formatting | bytes 5242880
  82.2 0.1 copy-done.5
  82.4 0.3 convolution_reduce_fusion.2
  82.7 2.2 all-gather
  84.8 2.8 %convolution_reduce_fusion.1 = f32[640]{0:T(1024)S(1)} fusion(f32[1280,1]{0,1:T(1,128)S(1)} %bitcast.161, bf16[640,1280]{1,0:T(8,128)(2,1)} %param.23), kind=kOutput, calls=%fused_computation.202 | convolution fusion | flops 9830400 | bytes 1646080 | tf_op jit(solution)/shard_map/dot_general | solution.py:97
  87.7 2.8 %convolution_reduce_fusion = f32[640]{0:T(1024)S(1)} fusion(f32[1280,1]{0,1:T(1,128)S(1)} %bitcast.162, bf16[640,1280]{1,0:T(8,128)(2,1)} %param.24), kind=kOutput, calls=%fused_computation.201 | convolution fusion | flops 9830400 | bytes 1646080 | tf_op jit(solution)/shard_map/dot_general | solution.py:100
  90.6 0.1 broadcast_in_dim.8
  90.8 6.2 %convolution_bitcast_fusion.16 = f32[640,1024]{0,1:T(8,128)} fusion(bf16[1280,1024]{0,1:T(8,128)(2,1)} %all-gather.3.cloned.1.call-done, bf16[9,640,1280]{2,1,0:T(8,128)(2,1)} %param.20), kind=kOutput, calls=%fused_computation.137 | convolution fusion | flops 1677721600 | bytes 6881280 | tf_op jit(solution)/shard_map/dot_general | solution.py:52
  97.0 5.3 %convolution_bitcast_fusion.17 = f32[640,1024]{0,1:T(8,128)} fusion(bf16[1280,1024]{0,1:T(8,128)(2,1)S(1)} %copy-done.9, bf16[9,640,1280]{2,1,0:T(8,128)(2,1)} %param.20), kind=kOutput, calls=%fused_computation.138 | convolution fusion | flops 1677721600 | bytes 6881280 | tf_op jit(solution)/shard_map/dot_general | solution.py:52
  102.3 5.3 %convolution_bitcast_fusion.18 = f32[640,1024]{0,1:T(8,128)} fusion(bf16[1280,1024]{0,1:T(8,128)(2,1)S(1)} %copy-done.9, bf16[9,640,1280]{2,1,0:T(8,128)(2,1)} %param.20), kind=kOutput, calls=%fused_computation.139 | convolution fusion | flops 1677721600 | bytes 6881280 | tf_op jit(solution)/shard_map/dot_general | solution.py:52
  107.6 3.8 %convolution_bitcast_fusion.19 = f32[640,1024]{0,1:T(8,128)} fusion(bf16[1280,1024]{0,1:T(8,128)(2,1)S(1)} %copy-done.9, bf16[9,640,1280]{2,1,0:T(8,128)(2,1)S(1)} %bitcast.166), kind=kOutput, calls=%fused_computation.140 | convolution fusion | flops 1677721600 | bytes 6881280 | tf_op jit(solution)/shard_map/dot_general | solution.py:52
  111.4 3.8 %convolution_bitcast_fusion.20 = f32[640,1024]{0,1:T(8,128)} fusion(bf16[1280,1024]{0,1:T(8,128)(2,1)S(1)} %copy-done.9, bf16[9,640,1280]{2,1,0:T(8,128)(2,1)S(1)} %bitcast.166), kind=kOutput, calls=%fused_computation.141 | convolution fusion | flops 1677721600 | bytes 6881280 | tf_op jit(solution)/shard_map/dot_general | solution.py:52
  115.2 3.7 %convolution_bitcast_fusion.21 = f32[640,1024]{0,1:T(8,128)} fusion(bf16[1280,1024]{0,1:T(8,128)(2,1)S(1)} %copy-done.9, bf16[9,640,1280]{2,1,0:T(8,128)(2,1)S(1)} %bitcast.166), kind=kOutput, calls=%fused_computation.142 | convolution fusion | flops 1677721600 | bytes 6881280 | tf_op jit(solution)/shard_map/dot_general | solution.py:52
  118.9 3.8 %convolution_bitcast_fusion.22 = f32[640,1024]{0,1:T(8,128)} fusion(bf16[1280,1024]{0,1:T(8,128)(2,1)S(1)} %copy-done.9, bf16[9,640,1280]{2,1,0:T(8,128)(2,1)S(1)} %bitcast.166), kind=kOutput, calls=%fused_computation.143 | convolution fusion | flops 1677721600 | bytes 6881280 | tf_op jit(solution)/shard_map/dot_general | solution.py:52
  122.7 3.7 %convolution_bitcast_fusion.23 = f32[640,1024]{0,1:T(8,128)} fusion(bf16[1280,1024]{0,1:T(8,128)(2,1)S(1)} %copy-done.9, bf16[9,640,1280]{2,1,0:T(8,128)(2,1)S(1)} %bitcast.166), kind=kOutput, calls=%fused_computation.144 | convolution fusion | flops 1677721600 | bytes 6881280 | tf_op jit(solution)/shard_map/dot_general | solution.py:52
  126.4 9.9 %fusion.51 = bf16[640,1024]{0,1:T(8,128)(2,1)S(1)} fusion(f32[640,1024]{0,1:T(8,128)} %convolution_bitcast_fusion.23, f32[640,1024]{0,1:T(8,128)} %convolution_bitcast_fusion.22, f32[640,1024]{0,1:T(8,128)} %convolution_bitcast_fusion.21, f32[640,1024]{0,1:T(8,128)} %convolution_bitcast_fusion.20, f32[640,1024]{0,1:T(8,128)} %convolution_bitcast_fusion.19, ...), kind=kOutput, calls=%fused_computation.99 | convolution fusion | flops 1690173440 | bytes 26583040 | tf_op jit(solution)/shard_map/dot_general | solution.py:52
  136.3 1.1 copy-done.3
  137.4 0.2 convert_reduce_fusion.2
  137.7 0.1 reduce_sum.83
  137.9 0.1 sub.167
  138.0 1.7 fusion.77
  139.8 0.1 reduce_sum.89
  140.0 0.1 mul.384
  140.1 7.0 %fusion.102 = f32[1024,1280]{1,0:T(8,128)} fusion(bf16[9,640,1280]{2,1,0:T(8,128)(2,1)} %param.21, bf16[640,1024]{0,1:T(8,128)(2,1)} %copy-done.3, f32[640]{0:T(1024)S(1)} %get-tuple-element.10, f32[640]{0:T(1024)S(1)} %get-tuple-element.11, f32[640]{0:T(1024)S(1)} %mul.384, f32[640]{0:T(1024)S(1)} %sub.167), kind=kOutput, calls=%fused_computation.158 | convolution fusion | flops 1684275200 | bytes 8202240 | tf_op jit(solution)/shard_map/dot_general | solution.py:60
  147.2 6.6 %convolution_bitcast_fusion.8 = f32[1280,1024]{0,1:T(8,128)} fusion(bf16[9,640,1280]{2,1,0:T(8,128)(2,1)} %param.21, bf16[640,1024]{0,1:T(8,128)(2,1)S(1)} %copy-done.4, f32[640]{0:T(1024)S(1)} %get-tuple-element.10, f32[640]{0:T(1024)S(1)} %get-tuple-element.11, f32[640]{0:T(1024)S(1)} %mul.384, f32[640]{0:T(1024)S(1)} %sub.167), kind=kOutput, calls=%fused_computation.59 | convolution fusion | flops 1684275200 | bytes 8202240 | tf_op jit(solution)/shard_map/dot_general | solution.py:60
  153.8 5.0 %convolution_bitcast_fusion.9 = f32[1280,1024]{0,1:T(8,128)} fusion(bf16[9,640,1280]{2,1,0:T(8,128)(2,1)S(1)} %bitcast.168, bf16[640,1024]{0,1:T(8,128)(2,1)S(1)} %copy-done.4, f32[640]{0:T(1024)S(1)} %get-tuple-element.10, f32[640]{0:T(1024)S(1)} %get-tuple-element.11, f32[640]{0:T(1024)S(1)} %mul.384, f32[640]{0:T(1024)S(1)} %sub.167), kind=kOutput, calls=%fused_computation.60 | convolution fusion | flops 1684275200 | bytes 8208384 | tf_op jit(solution)/shard_map/dot_general | solution.py:60
  158.8 5.0 %convolution_bitcast_fusion.10 = f32[1280,1024]{0,1:T(8,128)} fusion(bf16[9,640,1280]{2,1,0:T(8,128)(2,1)S(1)} %bitcast.168, bf16[640,1024]{0,1:T(8,128)(2,1)S(1)} %copy-done.4, f32[640]{0:T(1024)S(1)} %get-tuple-element.10, f32[640]{0:T(1024)S(1)} %get-tuple-element.11, f32[640]{0:T(1024)S(1)} %mul.384, f32[640]{0:T(1024)S(1)} %sub.167), kind=kOutput, calls=%fused_computation.61 | convolution fusion | flops 1684275200 | bytes 8208384 | tf_op jit(solution)/shard_map/dot_general | solution.py:60
  163.8 5.3 %convolution_bitcast_fusion.11 = f32[1280,1024]{0,1:T(8,128)} fusion(bf16[9,640,1280]{2,1,0:T(8,128)(2,1)S(1)} %bitcast.168, bf16[640,1024]{0,1:T(8,128)(2,1)S(1)} %copy-done.4, f32[640]{0:T(1024)S(1)} %get-tuple-element.10, f32[640]{0:T(1024)S(1)} %get-tuple-element.11, f32[640]{0:T(1024)S(1)} %mul.384, f32[640]{0:T(1024)S(1)} %sub.167), kind=kOutput, calls=%fused_computation.62 | convolution fusion | flops 1684275200 | bytes 8208384 | tf_op jit(solution)/shard_map/dot_general | solution.py:60
  169.2 5.1 %convolution_bitcast_fusion.12 = f32[1280,1024]{0,1:T(8,128)} fusion(bf16[9,640,1280]{2,1,0:T(8,128)(2,1)S(1)} %bitcast.168, bf16[640,1024]{0,1:T(8,128)(2,1)S(1)} %copy-done.4, f32[640]{0:T(1024)S(1)} %get-tuple-element.10, f32[640]{0:T(1024)S(1)} %get-tuple-element.11, f32[640]{0:T(1024)S(1)} %mul.384, f32[640]{0:T(1024)S(1)} %sub.167), kind=kOutput, calls=%fused_computation.63 | convolution fusion | flops 1684275200 | bytes 8208384 | tf_op jit(solution)/shard_map/dot_general | solution.py:60
  174.2 5.0 %convolution_bitcast_fusion.13 = f32[1280,1024]{0,1:T(8,128)} fusion(bf16[9,640,1280]{2,1,0:T(8,128)(2,1)S(1)} %bitcast.168, bf16[640,1024]{0,1:T(8,128)(2,1)S(1)} %copy-done.4, f32[640]{0:T(1024)S(1)} %get-tuple-element.10, f32[640]{0:T(1024)S(1)} %get-tuple-element.11, f32[640]{0:T(1024)S(1)} %mul.384, f32[640]{0:T(1024)S(1)} %sub.167), kind=kOutput, calls=%fused_computation.64 | convolution fusion | flops 1684275200 | bytes 8208384 | tf_op jit(solution)/shard_map/dot_general | solution.py:60
  179.2 5.1 %convolution_bitcast_fusion.14 = f32[1280,1024]{0,1:T(8,128)} fusion(bf16[9,640,1280]{2,1,0:T(8,128)(2,1)S(1)} %bitcast.168, bf16[640,1024]{0,1:T(8,128)(2,1)S(1)} %copy-done.4, f32[640]{0:T(1024)S(1)} %get-tuple-element.10, f32[640]{0:T(1024)S(1)} %get-tuple-element.11, f32[640]{0:T(1024)S(1)} %mul.384, f32[640]{0:T(1024)S(1)} %sub.167), kind=kOutput, calls=%fused_computation.65 | convolution fusion | flops 1684275200 | bytes 8208384 | tf_op jit(solution)/shard_map/dot_general | solution.py:60
  184.3 5.1 %convolution_bitcast_fusion.15 = f32[1280,1024]{0,1:T(8,128)} fusion(bf16[9,640,1280]{2,1,0:T(8,128)(2,1)S(1)} %bitcast.168, bf16[640,1024]{0,1:T(8,128)(2,1)S(1)} %copy-done.4, f32[640]{0:T(1024)S(1)} %get-tuple-element.10, f32[640]{0:T(1024)S(1)} %get-tuple-element.11, f32[640]{0:T(1024)S(1)} %mul.384, f32[640]{0:T(1024)S(1)} %sub.167), kind=kOutput, calls=%fused_computation.66 | convolution fusion | flops 1684275200 | bytes 8208384 | tf_op jit(solution)/shard_map/dot_general | solution.py:60
  189.4 2.4 copy.27
  191.8 19.4 %fusion.10 = bf16[1280,1024]{0,1:T(8,128)(2,1)} fusion(f32[1280,1024]{0,1:T(8,128)} %convolution_bitcast_fusion.15, f32[1280,1024]{0,1:T(8,128)} %convolution_bitcast_fusion.14, f32[1280,1024]{0,1:T(8,128)} %convolution_bitcast_fusion.13, f32[1280,1024]{0,1:T(8,128)} %convolution_bitcast_fusion.12, f32[1280,1024]{0,1:T(8,128)} %convolution_bitcast_fusion.11, ...), kind=kOutput, calls=%fused_computation.26 | convolution fusion | flops 1707212800 | bytes 54110720 | tf_op jit(solution)/shard_map/dot_general | solution.py:124
  211.2 4.5 %copy.28 = bf16[1280,1024]{1,0:T(8,128)(2,1)} copy(bf16[1280,1024]{0,1:T(8,128)(2,1)} %fusion.10) | data formatting | bytes 5242880
  215.7 13.7 %reduce-scatter.9.cloned.1.call-done = bf16[640,1024]{1,0:T(8,128)(2,1)} async-done(((bf16[1280,1024]{1,0:T(8,128)(2,1)}), bf16[640,1024]{1,0:T(8,128)(2,1)}) %reduce-scatter.9.cloned.1.call-update) | async-done | bytes 1310736
  229.5 2.4 %copy.29 = bf16[640,1024]{0,1:T(8,128)(2,1)} copy(bf16[640,1024]{1,0:T(8,128)(2,1)} %reduce-scatter.9.cloned.1.call-done) | data formatting | bytes 2621440
  231.9 2.7 %fusion.86 = bf16[640,1024]{0,1:T(8,128)(2,1)} fusion(bf16[640,1024]{0,1:T(8,128)(2,1)S(1)} %copy-done.2, bf16[640,1024]{0,1:T(8,128)(2,1)} %copy.29), kind=kLoop, calls=%fused_computation.134 | loop fusion | flops 2621440 | bytes 3932160 | tf_op jit(solution)/shard_map/convert_element_type | solution.py:134
  234.6 2.4 copy.25
  (83 shorter events, 1.5 us)
Async XLA Ops:
  6.5 185.3 %copy-start = (bf16[640,1280]{1,0:T(8,128)(2,1)S(1)}, bf16[640,1280]{1,0:T(8,128)(2,1)}, u32[]{:S(2)}) copy-start(bf16[640,1280]{1,0:T(8,128)(2,1)} %param.25) | copy-start | bytes 4915204
  6.5 3.3 %copy-start.7 = (f32[3,640]{1,0:T(4,128)S(1)}, f32[3,640]{1,0:T(4,128)}, u32[]{:S(2)}) copy-start(f32[3,640]{1,0:T(4,128)} %param.18) | copy-start | bytes 23044
  6.5 3.3 %copy-start.6 = (f32[3,640]{1,0:T(4,128)S(1)}, f32[3,640]{1,0:T(4,128)}, u32[]{:S(2)}) copy-start(f32[3,640]{1,0:T(4,128)} %param.19) | copy-start | bytes 23044
  6.5 84.2 %all-gather.3.cloned.1.call-start = ((), (), s32[]{:S(2)}) async-start(), calls=%async_computation.2 | async-start | bytes 3932160 | tf_op jit(solution)/shard_map/all_gather | solution.py:108
  8.4 3.5 %copy-start.1 = (bf16[640,1024]{0,1:T(8,128)(2,1)}, bf16[640,1024]{0,1:T(8,128)(2,1)S(1)}, u32[]{:S(2)}) copy-start(bf16[640,1024]{0,1:T(8,128)(2,1)S(1)} %copy.23) | copy-start | bytes 3932164
  11.9 177.5 %reduce-scatter.7.cloned.1.call-start = ((), (), s32[]{:S(2)}) async-start(), calls=%async_computation.3 | async-start | bytes 3932160
  15.5 13.5 %slice-start = ((s8[14745600]{0:T(1024)(128)(4,1)}), s8[4194304]{0:T(1024)(128)(4,1)S(1)}, s32[]{:S(2)}) async-start(s8[14745600]{0:T(1024)(128)(4,1)} %bitcast.163), calls=%async_computation.5 | async-start | bytes 8388608
  15.6 13.5 %slice-start.1 = ((s8[14745600]{0:T(1024)(128)(4,1)}), s8[4194304]{0:T(1024)(128)(4,1)S(1)}, s32[]{:S(2)}) async-start(s8[14745600]{0:T(1024)(128)(4,1)} %bitcast.163), calls=%async_computation.6 | async-start | bytes 8388608
  22.3 6.8 %slice-start.2 = ((s8[14745600]{0:T(1024)(128)(4,1)}), s8[4194304]{0:T(1024)(128)(4,1)S(1)}, s32[]{:S(2)}) async-start(s8[14745600]{0:T(1024)(128)(4,1)} %bitcast.163), calls=%async_computation.7 | async-start | bytes 8388608
  22.3 6.8 %slice-start.3 = ((s8[14745600]{0:T(1024)(128)(4,1)}), s8[2162688]{0:T(1024)(128)(4,1)S(1)}, s32[]{:S(2)}) async-start(s8[14745600]{0:T(1024)(128)(4,1)} %bitcast.163), calls=%async_computation.8 | async-start | bytes 4325376
  81.3 1.0 copy-start.5
  81.3 9.2 %copy-start.8 = (s32[1,8,8]{2,1,0:T(8,128)S(1)}, s32[1,8,8]{2,1,0:T(8,128)}, u32[]{:S(2)}) copy-start(s32[1,8,8]{2,1,0:T(8,128)} %param.15) | copy-start | bytes 772
  81.4 148.1 %reduce-scatter.9.cloned.1.call-start = ((), (), s32[]{:S(2)}) async-start(), calls=%async_computation.4 | async-start | bytes 3932160
  90.8 6.3 %copy-start.9 = (bf16[1280,1024]{0,1:T(8,128)(2,1)S(1)}, bf16[1280,1024]{0,1:T(8,128)(2,1)}, u32[]{:S(2)}) copy-start(bf16[1280,1024]{0,1:T(8,128)(2,1)} %all-gather.3.cloned.1.call-done) | copy-start | bytes 7864324
  90.8 16.8 %slice-start.4 = ((s8[14745600]{0:T(1024)(128)(4,1)}), s8[4194304]{0:T(1024)(128)(4,1)S(1)}, s32[]{:S(2)}) async-start(s8[14745600]{0:T(1024)(128)(4,1)} %bitcast.165), calls=%async_computation.9 | async-start | bytes 8388608
  90.8 16.8 %slice-start.5 = ((s8[14745600]{0:T(1024)(128)(4,1)}), s8[4194304]{0:T(1024)(128)(4,1)S(1)}, s32[]{:S(2)}) async-start(s8[14745600]{0:T(1024)(128)(4,1)} %bitcast.165), calls=%async_computation.10 | async-start | bytes 8388608
  97.0 10.6 %slice-start.6 = ((s8[14745600]{0:T(1024)(128)(4,1)}), s8[4194304]{0:T(1024)(128)(4,1)S(1)}, s32[]{:S(2)}) async-start(s8[14745600]{0:T(1024)(128)(4,1)} %bitcast.165), calls=%async_computation.11 | async-start | bytes 8388608
  102.3 5.3 %slice-start.7 = ((s8[14745600]{0:T(1024)(128)(4,1)}), s8[2162688]{0:T(1024)(128)(4,1)S(1)}, s32[]{:S(2)}) async-start(s8[14745600]{0:T(1024)(128)(4,1)} %bitcast.165), calls=%async_computation.12 | async-start | bytes 4325376
  136.3 1.1 copy-start.3
  140.1 7.0 %copy-start.4 = (bf16[640,1024]{0,1:T(8,128)(2,1)S(1)}, bf16[640,1024]{0,1:T(8,128)(2,1)}, u32[]{:S(2)}) copy-start(bf16[640,1024]{0,1:T(8,128)(2,1)} %copy-done.3) | copy-start | bytes 3932164
  140.1 13.7 %slice-start.8 = ((s8[14745600]{0:T(1024)(128)(4,1)}), s8[4194304]{0:T(1024)(128)(4,1)S(1)}, s32[]{:S(2)}) async-start(s8[14745600]{0:T(1024)(128)(4,1)} %bitcast.167), calls=%async_computation.13 | async-start | bytes 8388608
  140.1 13.7 %slice-start.9 = ((s8[14745600]{0:T(1024)(128)(4,1)}), s8[4194304]{0:T(1024)(128)(4,1)S(1)}, s32[]{:S(2)}) async-start(s8[14745600]{0:T(1024)(128)(4,1)} %bitcast.167), calls=%async_computation.14 | async-start | bytes 8388608
  147.2 6.7 %slice-start.10 = ((s8[14745600]{0:T(1024)(128)(4,1)}), s8[4194304]{0:T(1024)(128)(4,1)S(1)}, s32[]{:S(2)}) async-start(s8[14745600]{0:T(1024)(128)(4,1)} %bitcast.167), calls=%async_computation.15 | async-start | bytes 8388608
  147.2 6.7 %slice-start.11 = ((s8[14745600]{0:T(1024)(128)(4,1)}), s8[2162688]{0:T(1024)(128)(4,1)S(1)}, s32[]{:S(2)}) async-start(s8[14745600]{0:T(1024)(128)(4,1)} %bitcast.167), calls=%async_computation.16 | async-start | bytes 4325376
  215.7 16.2 %copy-start.2 = (bf16[640,1024]{0,1:T(8,128)(2,1)S(1)}, bf16[640,1024]{0,1:T(8,128)(2,1)}, u32[]{:S(2)}) copy-start(bf16[640,1024]{0,1:T(8,128)(2,1)} %copy-done.1) | copy-start | bytes 3932164
Sparse Core Ops, SparseCore 0:
  12.0 14.0 all-gather.2
  81.5 13.1 reduce-scatter.6
  215.9 13.5 reduce-scatter.8
where the time goes:
time: 247 us; the launch traced here: 244 us
  matrix products  181 us (73%)
  local copies, waits for them, and re-layouts  23.4 us (9%)
  between operations  14.4 us (6%)
  waiting for transfers between devices  13.8 us (6%)
  other arithmetic  8.88 us (4%)
    dot_general x18, matrix products, conv_flipped(): lax.dot_general(weights[place], inputs, (((0,), (0,)), ((), ())), preferr...  110 us
    dot_general x9, matrix products, conv_plain(): jnp.dot(weights[place], inputs, preferred_element_type=jnp.float32)  45.4 us
    dot_general x1, matrix products, local(): lax.dot_general(weights, control_state, (((0,), (0,)), ((), ())), preferr...  19.4 us
    unnamed x51, local copies, waits for them, and re-layouts  19.2 us
    unnamed x5, waiting for transfers between devices  13.8 us
  transfers between devices with their start and end apart: 3, of which 1 were waited for; matrix products, arithmetic and copies ran while one was open for 71% of the time, Pallas kernels for 0%

commit v1 on v0

--- a/solution.py
+++ b/solution.py
@@ -1,8 +1,12 @@
+import functools
 import math
 
 import jax
 import jax.numpy as jnp
+import numpy as np
 from jax import lax
+from jax.experimental import pallas as pl
+from jax.experimental.pallas import tpu as pltpu
 from jax.sharding import PartitionSpec as P
 
 C = 1280
@@ -12,12 +16,435 @@
 TILE = 4
 VIEWS = 1
 
+BF = jnp.bfloat16
+F32 = jnp.float32
+WIDE = 256
+LANES = 128
+CHUNK = 2 * S
+
 
 def timestep_features(timestep):
     half_width = FREQ // 2
     rates = jnp.exp(-math.log(10000.0) * jnp.arange(half_width, dtype=jnp.float32) / half_width)
     angles = timestep.astype(jnp.float32)[0] * rates
     return jnp.concatenate([jnp.cos(angles), jnp.sin(angles)])
+
+
+def half_silu(v):
+    h = 0.5 * v
+    return h + h * jnp.tanh(h)
+
+
+def group_masks(channels, size):
+    groups = channels // size
+    row = lax.broadcasted_iota(jnp.int32, (groups, channels), 0)
+    col = lax.broadcasted_iota(jnp.int32, (groups, channels), 1)
+    return ((col >= row * size) & (col < row * size + size)).astype(F32)
+
+
+def group_mean(sums, mask, count):
+    per_group = jnp.sum(mask * sums, axis=1, keepdims=True) * (1.0 / count)
+    return jnp.sum(mask * per_group, axis=0, keepdims=True)
+
+
+def norm_rows(xt, size, gain):
+    cells, channels = xt.shape
+    mask = group_masks(channels, size)
+
+    def fold(value):
+        return jnp.sum(value.reshape(CHUNK // 8, 8, channels), axis=0)
+
+    def add(i, total):
+        return total + fold(xt[pl.ds(pl.multiple_of(i * CHUNK, CHUNK), CHUNK), :].astype(F32))
+
+    total = lax.fori_loop(0, cells // CHUNK, add, jnp.zeros((8, channels), F32))
+    mean = group_mean(jnp.sum(total, axis=0, keepdims=True), mask, cells * size)
+
+    def add_square(i, total):
+        d = xt[pl.ds(pl.multiple_of(i * CHUNK, CHUNK), CHUNK), :].astype(F32) - mean
+        return total + fold(d * d)
+
+    total = lax.fori_loop(0, cells // CHUNK, add_square, jnp.zeros((8, channels), F32))
+    variance = group_mean(jnp.sum(total, axis=0, keepdims=True), mask, cells * size)
+    return mean, lax.rsqrt(variance + 1e-05) * gain
+
+
+def turn_in(x_ref, xt):
+    channels = x_ref.shape[0]
+    for b in range(channels // LANES):
+        part = slice(b * LANES, (b + 1) * LANES)
+        xt[:, part] = x_ref[part, :].astype(F32).T.astype(BF)
+
+
+def edge_masks(rows, channels):
+    col = lax.broadcasted_iota(jnp.int32, (rows, channels), 0) % S
+    return col != 0, col != S - 1
+
+
+def store_shifted(sh, start, y, left_ok, right_ok, offset=0):
+    rows, channels = y.shape
+    width = sh.shape[1] // 3
+    lo = jnp.where(left_ok, pltpu.roll(y, 1, 0), 0.0)
+    hi = jnp.where(right_ok, pltpu.roll(y, rows - 1, 0), 0.0)
+    for k, v in enumerate((lo, y, hi)):
+        sh[pl.ds(start, rows), k * width + offset:k * width + offset + channels] = v.astype(BF)
+
+
+def clear_border(sh):
+    blank = jnp.zeros((S, sh.shape[1]), sh.dtype)
+    sh[0:S, :] = blank
+    sh[sh.shape[0] - S:, :] = blank
+
+
+def stage_first(x_ref, gain_ref, bias_ref, step_ref, rate_ref, tw_ref, o_ref, tv_ref, xt, *, size):
+    cells, channels = o_ref.shape
+    turn_in(x_ref, xt)
+    mean, scale = norm_rows(xt, size, gain_ref[0:1, :])
+    bias = bias_ref[0:1, :]
+
+    def body(i, _):
+        rows = pl.ds(pl.multiple_of(i * CHUNK, CHUNK), CHUNK)
+        y = half_silu((xt[rows, :].astype(F32) - mean) * scale + bias)
+        o_ref[rows, :] = y.astype(BF)
+        return 0
+
+    lax.fori_loop(0, cells // CHUNK, body, 0)
+    angle = step_ref[0].astype(F32) * rate_ref[...]
+    row = lax.broadcasted_iota(jnp.int32, angle.shape, 0)
+    features = jnp.where(row < angle.shape[0] // 2, jnp.cos(angle), jnp.sin(angle))
+    total = jnp.sum(tw_ref[...].astype(F32) * features, axis=0, keepdims=True)
+    tv_ref[...] = total / (1.0 + jnp.exp(-total))
+
+
+def stage_control(index_ref, x_ref, gain_ref, bias_ref, w_ref, far_ref, near_ref, xt, sh, *, size):
+    cells = x_ref.shape[1]
+    channels = x_ref.shape[0]
+    j = pl.program_id(0)
+
+    @pl.when(j == 0)
+    def _():
+        clear_border(sh)
+        turn_in(x_ref, xt)
+        mean, scale = norm_rows(xt, size, gain_ref[2:3, :])
+        bias = bias_ref[2:3, :]
+        left_ok, right_ok = edge_masks(CHUNK, channels)
+
+        def body(i, _):
+            start = pl.multiple_of(i * CHUNK, CHUNK)
+            y = half_silu((xt[pl.ds(start, CHUNK), :].astype(F32) - mean) * scale + bias)
+            store_shifted(sh, pl.multiple_of(start + S, S), y, left_ok, right_ok)
+            return 0
+
+        lax.fori_loop(0, cells // CHUNK, body, 0)
+
+    lhs = jnp.concatenate([sh[S * dy:S * dy + cells, :] for dy in range(3)], axis=1)
+    rhs = w_ref[...].reshape(w_ref.shape[0] * w_ref.shape[1], WIDE)
+    product = jnp.dot(lhs, rhs, preferred_element_type=F32)
+    for half in range(WIDE // LANES):
+        value = product[:, half * LANES:(half + 1) * LANES]
+        block = (2 * j + half) - index_ref[0] * (channels // LANES)
+        inside = (block >= 0) & (block < channels // LANES)
+
+        @pl.when(inside)
+        def _():
+            cols = pl.ds(pl.multiple_of(block * LANES, LANES), LANES)
+            near_ref[:, cols] = value + xt[:, cols].astype(F32)
+
+        @pl.when(jnp.logical_not(inside))
+        def _():
+            other = (2 * j + half) - (1 - index_ref[0]) * (channels // LANES)
+            far_ref[:, pl.ds(pl.multiple_of(other * LANES, LANES), LANES)] = value.astype(BF)
+
+
+def stage_hidden(index_ref, own_ref, got_ref, tv_ref, tvgot_ref, gain_ref, bias_ref, ut_ref, ct_ref, w_ref,
+                 sh_ref, shift_ref, xs, acc, ushift, *, size):
+    cells, channels = own_ref.shape
+    s = pl.program_id(0)
+    me = index_ref[0]
+    mine = pl.ds(pl.multiple_of(me * channels, LANES), channels)
+    theirs = pl.ds(pl.multiple_of((1 - me) * channels, LANES), channels)
+
+    @pl.when(s == 0)
+    def _():
+        clear_border(xs)
+        xs[S:S + cells, mine] = own_ref[...]
+        xs[S:S + cells, theirs] = got_ref[...]
+
+    def time_column(t_ref):
+        a = jnp.sum(t_ref[:, mine].astype(F32) * tv_ref[...], axis=1, keepdims=True)
+        return a + jnp.sum(t_ref[:, theirs].astype(F32) * tvgot_ref[...], axis=1, keepdims=True)
+
+    @pl.when(s == 0)
+    def _():
+        ushift[...] = jnp.broadcast_to(time_column(ut_ref), ushift.shape)
+        column = jnp.broadcast_to(time_column(ct_ref), (channels, LANES))
+        for b in range(channels // LANES):
+            part = slice(b * LANES, (b + 1) * LANES)
+            shift_ref[:, part] = column[part, :].T[0:8, :]
+
+    weights = jnp.concatenate([w_ref[k, 0] for k in range(3)], axis=1)
+    col = lax.broadcasted_iota(jnp.int32, (8, WIDE), 1) % S
+    for cb in range(cells // WIDE):
+        rhs = jnp.concatenate([xs[S * dy + cb * WIDE:S * dy + cb * WIDE + WIDE, :] for dy in range(3)], axis=1)
+        p = lax.dot_general(weights, rhs, (((1,), (1,)), ((), ())), preferred_element_type=F32)
+        part = slice(cb * WIDE, (cb + 1) * WIDE)
+
+        @pl.when(s == 0)
+        def _():
+            acc[:, part] = p
+
+        @pl.when(s == 1)
+        def _():
+            moved = pltpu.roll(p, 1, 1).reshape(channels // 8, 8, WIDE)
+            acc[:, part] += jnp.where((col != 0)[None], moved, 0.0).reshape(channels, WIDE)
+
+        @pl.when(s == 2)
+        def _():
+            moved = pltpu.roll(p, WIDE - 1, 1).reshape(channels // 8, 8, WIDE)
+            acc[:, part] += jnp.where((col != S - 1)[None], moved, 0.0).reshape(channels, WIDE)
+
+    @pl.when(s == 2)
+    def _():
+        clear_border(sh_ref)
+        count = 1.0 / (cells * size)
+
+        def norm(g, _):
+            rows = pl.ds(pl.multiple_of(g * size, 8), size)
+            h = (acc[rows, :] + ushift[rows, 0:1]).astype(BF).astype(F32)
+            mean = jnp.sum(jnp.sum(h, axis=0, keepdims=True), axis=1, keepdims=True) * count
+            d = h - mean
+            variance = jnp.sum(jnp.sum(d * d, axis=0, keepdims=True), axis=1, keepdims=True) * count
+            scale = lax.rsqrt(variance + 1e-05) * gain_ref[rows, 1:2]
+            acc[rows, :] = half_silu(d * scale + bias_ref[rows, 1:2])
+            return 0
+
+        lax.fori_loop(0, channels // size, norm, 0)
+        left_ok, right_ok = edge_masks(WIDE, LANES)
+        for b in range(channels // LANES):
+            for cb in range(cells // WIDE):
+                y = acc[b * LANES:(b + 1) * LANES, cb * WIDE:(cb + 1) * WIDE].T
+                store_shifted(sh_ref, S + cb * WIDE, y, left_ok, right_ok, offset=b * LANES)
+
+
+def gated_state(near_ref, got_ref, shift_ref, mask_ref, state):
+    cells, channels = state.shape
+    band = TILE * S
+    where = lax.broadcasted_iota(jnp.int32, (band, channels), 0) % S // TILE
+
+    def body(i, _):
+        rows = pl.ds(pl.multiple_of(i * band, band), band)
+        value = (near_ref[rows, :] + got_ref[rows, :].astype(F32) + shift_ref[0:1, :]).astype(BF).astype(F32)
+        gate = jnp.zeros((band, channels), F32)
+        for t in range(S // TILE):
+            gate = jnp.where(where == t, mask_ref[i, t].astype(F32), gate)
+        state[rows, :] = (value * gate).astype(BF)
+        return 0
+
+    lax.fori_loop(0, cells // band, body, 0)
+
+
+def out_product(sh_ref, state, w_ref, z_ref):
+    cells = state.shape[0]
+    lhs = jnp.concatenate([sh_ref[S * dy:S * dy + cells, :] for dy in range(3)] + [state[...]], axis=1)
+    rhs = jnp.concatenate([w_ref[...].reshape(w_ref.shape[0] * w_ref.shape[1], WIDE), z_ref[...]], axis=0)
+    return jnp.dot(lhs, rhs, preferred_element_type=F32)
+
+
+def stage_far(index_ref, mask_ref, sh_ref, near_ref, got_ref, shift_ref, w_ref, z_ref, far_ref, mixed_ref, state_ref):
+    cells, channels = near_ref.shape
+    j = pl.program_id(0)
+
+    @pl.when(j == 0)
+    def _():
+        gated_state(near_ref, got_ref, shift_ref, mask_ref, state_ref)
+
+    product = out_product(sh_ref, state_ref, w_ref, z_ref)
+    for half in range(WIDE // LANES):
+        value = product[:, half * LANES:(half + 1) * LANES]
+        block = 2 * j + half - (1 - index_ref[0])
+        inside = (block >= 0) & (block < channels // LANES)
+
+        @pl.when(inside)
+        def _():
+            far_ref[:, pl.ds(pl.multiple_of(block * LANES, LANES), LANES)] = value.astype(BF)
+
+        @pl.when(jnp.logical_not(inside))
+        def _():
+            mixed_ref[...] = value
+
+
+def stage_near(index_ref, sh_ref, state_ref, w_ref, z_ref, o_ref):
+    o_ref[...] = out_product(sh_ref, state_ref, w_ref, z_ref)
+
+
+def stage_last(index_ref, x_ref, near_ref, mixed_ref, got_ref, o_ref):
+    b = pl.program_id(0)
+    is_mixed = b == jnp.where(index_ref[0] == 0, pl.num_programs(0) - 1, 0)
+    local = jnp.where(is_mixed, mixed_ref[...], near_ref[...])
+    total = local + got_ref[...].astype(F32)
+    o_ref[...] = (x_ref[...].astype(F32) + total.T).astype(BF)
+
+
+def whole(shape):
+    return pl.BlockSpec(shape, lambda *_: (0,) * len(shape), pipeline_mode=pl.Buffered(1))
+
+
+def params(mib):
+    return pltpu.CompilerParams(vmem_limit_bytes=mib << 20)
+
+
+def cost(flops, read):
+    return pl.CostEstimate(flops=flops, bytes_accessed=read, transcendentals=0)
+
+
+def local_pair(latent_x, control_h, tile_mask, timestep, time_weight, norm_gain, norm_bias, unet_conv_in,
+               unet_conv_out, control_conv, unet_temb, control_temb, zero_conv):
+    channels, cells = latent_x.shape
+    full = unet_conv_in.shape[2]
+    size = full // GROUPS
+    swap = [(0, 1), (1, 0)]
+    me = lax.axis_index("tensor").astype(jnp.int32).reshape(1)
+    half_width = FREQ // 2
+    rates = np.exp(-math.log(10000.0) * np.arange(half_width, dtype=np.float32) / half_width).astype(np.float32)
+    rates = jnp.asarray(np.concatenate([rates, rates])[:, None])
+    smem = pl.BlockSpec(memory_space=pltpu.SMEM)
+
+    first, time_own = pl.pallas_call(
+        functools.partial(stage_first, size=size),
+        name="first",
+        out_shape=(jax.ShapeDtypeStruct((cells, channels), BF), jax.ShapeDtypeStruct((1, channels), F32)),
+        in_specs=[pl.BlockSpec(memory_space=pltpu.VMEM)] * 3 + [smem] + [pl.BlockSpec(memory_space=pltpu.VMEM)] * 2,
+        out_specs=(pl.BlockSpec(memory_space=pltpu.VMEM),) * 2,
+        scratch_shapes=[pltpu.VMEM((cells, channels), BF)],
+        compiler_params=params(32),
+        cost_estimate=cost(20 * cells * channels, 4 * cells * channels),
+    )(latent_x, norm_gain, norm_bias, timestep, rates, time_weight)
+    first_got = lax.ppermute(first, "tensor", swap)
+    time_got = lax.ppermute(time_own, "tensor", swap)
+
+    taps = control_conv.shape[0]
+    conv_flops = 2 * taps * channels * full * cells
+    conv_bytes = 2 * taps * channels * full
+    control_far, control_near = pl.pallas_call(
+        functools.partial(stage_control, size=size),
+        name="control",
+        out_shape=(jax.ShapeDtypeStruct((cells, channels), BF), jax.ShapeDtypeStruct((cells, channels), F32)),
+        grid_spec=pltpu.PrefetchScalarGridSpec(
+            num_scalar_prefetch=1,
+            grid=(full // WIDE,),
+            in_specs=[
+                whole((channels, cells)),
+                whole(norm_gain.shape),
+                whole(norm_bias.shape),
+                pl.BlockSpec((taps, channels, WIDE), lambda j, i: (0, 0, j)),
+            ],
+            out_specs=(whole((cells, channels)), whole((cells, channels))),
+            scratch_shapes=[pltpu.VMEM((cells, channels), BF), pltpu.VMEM((cells + 2 * S, 3 * channels), BF)],
+        ),
+        compiler_params=params(40),
+        cost_estimate=cost(conv_flops, conv_bytes),
+    )(me, control_h, norm_gain, norm_bias, control_conv)
+    control_got = lax.ppermute(control_far, "tensor", swap)
+
+    columns = (norm_gain.T, norm_bias.T)
+    shifted, control_shift = pl.pallas_call(
+        functools.partial(stage_hidden, size=size),
+        name="hidden",
+        out_shape=(jax.ShapeDtypeStruct((cells + 2 * S, 3 * channels), BF), jax.ShapeDtypeStruct((8, channels), F32)),
+        grid_spec=pltpu.PrefetchScalarGridSpec(
+            num_scalar_prefetch=1,
+            grid=(3,),
+            in_specs=[
+                whole((cells, channels)),
+                whole((cells, channels)),
+                whole((1, channels)),
+                whole((1, channels)),
+                whole(columns[0].shape),
+                whole(columns[1].shape),
+                whole(unet_temb.shape),
+                whole(control_temb.shape),
+                pl.BlockSpec((3, 1, channels, full), lambda s, i: (0, jnp.where(s == 0, 1, jnp.where(s == 1, 0, 2)), 0, 0)),
+            ],
+            out_specs=(whole((cells + 2 * S, 3 * channels)), whole((8, channels))),
+            scratch_shapes=[
+                pltpu.VMEM((cells + 2 * S, full), BF),
+                pltpu.VMEM((channels, cells), F32),
+                pltpu.VMEM((channels, LANES), F32),
+            ],
+        ),
+        compiler_params=params(48),
+        cost_estimate=cost(conv_flops, conv_bytes),
+    )(me, first, first_got, time_own, time_got, *columns, unet_temb, control_temb,
+      unet_conv_in.reshape(3, 3, channels, full))
+
+    far_tiles = -(-channels // WIDE)
+    near_tiles = full // WIDE - far_tiles
+    mask = tile_mask.reshape(tile_mask.shape[1:])
+    far, mixed, state = pl.pallas_call(
+        stage_far,
+        name="far",
+        out_shape=(
+            jax.ShapeDtypeStruct((cells, channels), BF),
+            jax.ShapeDtypeStruct((cells, LANES), F32),
+            jax.ShapeDtypeStruct((cells, channels), BF),
+        ),
+        grid_spec=pltpu.PrefetchScalarGridSpec(
+            num_scalar_prefetch=1,
+            grid=(far_tiles,),
+            in_specs=[
+                smem,
+                whole((cells + 2 * S, 3 * channels)),
+                whole((cells, channels)),
+                whole((cells, channels)),
+                whole((8, channels)),
+                pl.BlockSpec((taps, channels, WIDE), lambda j, i: (0, 0, (1 - i[0]) * near_tiles + j)),
+                pl.BlockSpec((channels, WIDE), lambda j, i: (0, (1 - i[0]) * near_tiles + j)),
+            ],
+            out_specs=(whole((cells, channels)), whole((cells, LANES)), whole((cells, channels))),
+        ),
+        compiler_params=params(40),
+        cost_estimate=cost(conv_flops * far_tiles * WIDE // full, conv_bytes * far_tiles * WIDE // full),
+    )(me, mask, shifted, control_near, control_got, control_shift, unet_conv_out, zero_conv)
+    got = lax.ppermute(far, "tensor", swap)
+
+    near = pl.pallas_call(
+        stage_near,
+        name="near",
+        out_shape=jax.ShapeDtypeStruct((cells, near_tiles * WIDE), F32),
+        grid_spec=pltpu.PrefetchScalarGridSpec(
+            num_scalar_prefetch=1,
+            grid=(near_tiles,),
+            in_specs=[
+                whole((cells + 2 * S, 3 * channels)),
+                whole((cells, channels)),
+                pl.BlockSpec((taps, channels, WIDE), lambda j, i: (0, 0, i[0] * far_tiles + j)),
+                pl.BlockSpec((channels, WIDE), lambda j, i: (0, i[0] * far_tiles + j)),
+            ],
+            out_specs=pl.BlockSpec((cells, WIDE), lambda j, i: (0, j)),
+        ),
+        compiler_params=params(40),
+        cost_estimate=cost(conv_flops * near_tiles * WIDE // full, conv_bytes * near_tiles * WIDE // full),
+    )(me, shifted, state, unet_conv_out, zero_conv)
+
+    last_near = near_tiles * WIDE // LANES - 1
+    return pl.pallas_call(
+        stage_last,
+        name="last",
+        out_shape=jax.ShapeDtypeStruct((channels, cells), BF),
+        grid_spec=pltpu.PrefetchScalarGridSpec(
+            num_scalar_prefetch=1,
+            grid=(channels // LANES,),
+            in_specs=[
+                pl.BlockSpec((LANES, cells), lambda b, i: (b, 0)),
+                pl.BlockSpec((cells, LANES), lambda b, i: (0, jnp.clip(b - i[0], 0, last_near))),
+                whole((cells, LANES)),
+                pl.BlockSpec((cells, LANES), lambda b, i: (0, b)),
+            ],
+            out_specs=pl.BlockSpec((LANES, cells), lambda b, i: (b, 0)),
+        ),
+        compiler_params=params(24),
+        cost_estimate=cost(4 * channels * cells, 10 * channels * cells),
+    )(me, latent_x, near, mixed, got)
 
 
 def norm_silu(inputs, scales, shifts):
@@ -71,7 +498,7 @@
     return spread_mask.reshape(VIEWS * S * S)
 
 
-def local(
+def local_any(
     latent_x,
     control_h,
     tile_mask,
@@ -150,6 +577,12 @@
         P("tensor", None),
         P("tensor", None),
     )
+
+    def local(latent_x, *rest):
+        channels, cells = latent_x.shape
+        paired = mesh.shape["tensor"] == 2 and channels % WIDE == LANES and VIEWS == 1 and cells == S * S
+        return (local_pair if paired else local_any)(latent_x, *rest)
+
     return jax.shard_map(
         local, mesh=mesh, in_specs=placed, out_specs=P("tensor", "dp"), check_vma=False
     )

time: 247 us -> 114 us (0.46)
  matrix products: 181 us -> 0 us
  Pallas kernels: 0 us -> 101 us
  waiting for transfers between devices: 13.8 us -> 0.01 us
  between operations: 14.4 us -> 0.79 us
  local copies, waits for them, and re-layouts: 23.4 us -> 10 us
  other arithmetic: 8.88 us -> 0 us
    dot_general x31 -> x0, matrix products: 181 us -> none  [the longest x18 110 us: conv_flipped(): lax.dot_general(weights[place], inputs, (((0,), (0,)), ((), ())), preferr...]
    pallas_call x0 -> x6, Pallas kernels: none -> 101 us  [the longest x1 48.7 us: local_pair(): pl.pallas_call(functools.partial(stage_hidden, size=size), name='hidden',...]
    unnamed x5 -> x0, waiting for transfers between devices: 13.8 us -> none
    unnamed x51 -> x32, local copies, waits for them, and re-layouts: 19.2 us -> 10 us
    convert_element_type x7 -> x0, other arithmetic: 4.74 us -> none  [the longest x1 2.7 us: local(): return (latent_x.astype(jnp.float32) + combined).astype(jnp.bfloat16)]
    reduce_sum x12 -> x0, other arithmetic: 3.96 us -> none  [the longest x6 2.87 us: norm_silu(): variance = jnp.mean(centred * centred, axis=(1, 3), keepdims=True)]
  transfers between devices with their start and end apart: 3 -> 4, of which waited for: 1 -> 0; matrix products, arithmetic and copies ran while one was open for 71% -> 0% of each run, Pallas kernels for 0% -> 71%
where the time goes in v1:
time: 114 us; the launch traced here: 113 us
  Pallas kernels  101 us (89%)
  local copies, waits for them, and re-layouts  10 us (9%)
    pallas_call x1, Pallas kernels, local_pair(): pl.pallas_call(functools.partial(stage_hidden, size=size), name='hidden',...  48.7 us
    pallas_call x1, Pallas kernels, local_pair(): pl.pallas_call(functools.partial(stage_control, size=size), name='control...  22.7 us
    pallas_call x1, Pallas kernels, local_pair(): pl.pallas_call(stage_far, name='far', out_shape=(jax.ShapeDtypeStruct((ce...  14 us
    unnamed x32, local copies, waits for them, and re-layouts  10 us
    pallas_call x1, Pallas kernels, local_pair(): pl.pallas_call(stage_near, name='near', out_shape=jax.ShapeDtypeStruct((c...  9.23 us
    pallas_call x1, Pallas kernels, local_pair(): pl.pallas_call(functools.partial(stage_first, size=size), name='first', o...  3.3 us
    pallas_call x1, Pallas kernels, local_pair(): pl.pallas_call(stage_last, name='last', out_shape=jax.ShapeDtypeStruct((c...  3.16 us
  transfers between devices with their start and end apart: 4, of which 0 were waited for; matrix products, arithmetic and copies ran while one was open for 0% of the time, Pallas kernels for 71%

profile of v1, /device:TPU:0, one launch (start us, length us, event | category | flops | bytes accessed | tf_op | source)
XLA Modules:
  0.0 113.1 jit_solution(8973478592673818403)
XLA Ops:
  0.7 0.0 copy-start
  0.7 1.3 %copy-done = bf16[640,1024]{1,0:T(8,128)(2,1)S(1)} copy-done((bf16[640,1024]{1,0:T(8,128)(2,1)S(1)}, bf16[640,1024]{1,0:T(8,128)(2,1)}, u32[]{:S(2)}) %copy-start) | copy-done | bytes 1310744
  2.0 0.0 copy-start.4
  2.0 1.0 copy-done.4
  3.0 0.0 copy-start.5
  3.0 0.9 copy-done.5
  3.9 0.0 copy-start.6
  3.9 0.7 copy-done.6
  4.6 0.0 copy-start.8
  4.6 0.7 copy-done.8
  5.3 0.0 copy-start.7
  5.3 0.0 copy-start.9
  5.3 3.3 %first.1 = (bf16[1024,640]{1,0:T(8,128)(2,1)}, f32[1,640]{1,0:T(1,128)S(1)}) custom-call(bf16[640,1024]{1,0:T(8,128)(2,1)S(1)} %copy-done, f32[3,640]{1,0:T(4,128)S(1)} %copy-done.6, f32[3,640]{1,0:T(4,128)S(1)} %copy-done.8, s32[1]{0:T(128)S(6)} %copy.17.step_ref, f32[320,1]{1,0:T(8,128)S(1)} %copy-done.5, bf16[320,640]{1,0:T(8,128)(2,1)S(1)} %copy-done.4), custom_call_target="tpu_custom_call" | custom-call | flops 13107200 | bytes 2621440 | tf_op jit(solution)/shard_map/first/pallas_call | solution.py:312
  8.6 0.5 collective-permute-start.1
  9.1 0.0 collective-permute-start
  9.1 0.0 copy-done.7
  9.1 0.0 copy-done.9
  9.1 0.0 copy-start.11
  9.1 1.3 %copy-done.11 = bf16[640,1024]{1,0:T(8,128)(2,1)S(1)} copy-done((bf16[640,1024]{1,0:T(8,128)(2,1)S(1)}, bf16[640,1024]{1,0:T(8,128)(2,1)}, u32[]{:S(2)}) %copy-start.11) | copy-done | bytes 1310744
  10.4 0.0 copy-start.10
  10.4 22.7 %control.1 = (bf16[1024,640]{1,0:T(8,128)(2,1)}, f32[1024,640]{1,0:T(8,128)S(1)}) custom-call(s32[1]{0:T(128)} %bitcast.index_ref, bf16[640,1024]{1,0:T(8,128)(2,1)S(1)} %copy-done.11, f32[3,640]{1,0:T(4,128)S(1)} %copy-done.7, f32[3,640]{1,0:T(4,128)S(1)} %copy-done.9, bf16[9,640,1280]{2,1,0:T(8,128)(2,1)} %w_ref.3), custom_call_target="tpu_custom_call" | custom-call | flops 15099494400 | bytes 14745600 | tf_op jit(solution)/shard_map/control/pallas_call | solution.py:328
  33.2 0.0 copy-start.13
  33.2 1.5 %copy-done.13 = f32[1024,640]{1,0:T(8,128)} copy-done((f32[1024,640]{1,0:T(8,128)}, f32[1024,640]{1,0:T(8,128)S(1)}, u32[]{:S(2)}) %copy-start.13) | copy-done | bytes 2621464
  34.7 0.5 collective-permute-start.2
  35.2 0.2 copy.15
  35.4 0.2 copy.16
  35.6 0.0 collective-permute-done.1.tvgot_ref
  35.6 0.0 collective-permute-done.got_ref
  35.6 0.0 copy-done.10
  35.6 0.0 copy-start.3
  35.6 0.0 copy-start.12
  35.6 0.0 copy-start.14
  35.6 48.7 %hidden.1 = (bf16[1088,1920]{1,0:T(8,128)(2,1)}, f32[8,640]{1,0:T(8,128)S(1)}) custom-call(s32[1]{0:T(128)} %bitcast.index_ref, bf16[1024,640]{1,0:T(8,128)(2,1)} %get-tuple-element.14.own_ref, bf16[1024,640]{1,0:T(8,128)(2,1)} %collective-permute-done.got_ref, f32[1,640]{1,0:T(1,128)S(1)} %get-tuple-element.15.tv_ref, ...), custom_call_target="tpu_custom_call" | custom-call | flops 15099494400 | bytes 14745600 | tf_op jit(solution)/shard_map/hidden/pallas_call | solution.py:350
  84.4 0.0 collective-permute-done.2.got_ref
  84.4 0.0 copy-done.3
  84.4 0.0 copy-done.12
  84.4 0.0 copy-done.14
  84.4 0.0 copy-start.2
  84.4 2.2 %copy-done.2 = bf16[1088,1920]{1,0:T(8,128)(2,1)S(1)} copy-done((bf16[1088,1920]{1,0:T(8,128)(2,1)S(1)}, bf16[1088,1920]{1,0:T(8,128)(2,1)}, u32[]{:S(2)}) %copy-start.2) | copy-done | bytes 4177944
  86.6 14.0 %far.1 = (bf16[1024,640]{1,0:T(8,128)(2,1)S(1)}, f32[1024,128]{1,0:T(8,128)S(1)}, bf16[1024,640]{1,0:T(8,128)(2,1)S(1)}) custom-call(s32[1]{0:T(128)} %bitcast.index_ref, s32[8,8]{1,0:T(8,128)S(1)} %bitcast.7, bf16[1088,1920]{1,0:T(8,128)(2,1)S(1)} %copy-done.2, f32[1024,640]{1,0:T(8,128)S(1)} %copy-done.14, ...), custom_call_target="tpu_custom_call" | custom-call | flops 9059696640 | bytes 8847360 | tf_op jit(solution)/shard_map/far/pallas_call | solution.py:383
  100.6 0.1 collective-permute-start.3
  100.7 0.0 copy-start.1
  100.7 9.2 %near.1.near_ref = f32[1024,512]{1,0:T(8,128)S(1)} custom-call(s32[1]{0:T(128)} %bitcast.index_ref, bf16[1088,1920]{1,0:T(8,128)(2,1)S(1)} %copy-done.2, bf16[1024,640]{1,0:T(8,128)(2,1)S(1)} %get-tuple-element.20.state_ref, bf16[9,640,1280]{2,1,0:T(8,128)(2,1)} %w_ref.5, bf16[640,1280]{1,0:T(8,128)(2,1)S(1)} %copy-done.3), custom_call_target="tpu_custom_call" | custom-call | flops 6039797760 | bytes 5898240 | tf_op jit(solution)/shard_map/near/pallas_call | solution.py:410
  109.9 0.0 collective-permute-done.3.got_ref
  109.9 0.0 copy-done.1
  109.9 3.2 %last.1 = bf16[640,1024]{1,0:T(8,128)(2,1)} custom-call(s32[1]{0:T(128)} %bitcast.index_ref, bf16[640,1024]{1,0:T(8,128)(2,1)S(1)} %copy-done.1, f32[1024,512]{1,0:T(8,128)S(1)} %near.1.near_ref, f32[1024,128]{1,0:T(8,128)S(1)} %get-tuple-element.21.mixed_ref, bf16[1024,640]{1,0:T(8,128)(2,1)S(1)} %collective-permute-done.3.got_ref), custom_call_target="tpu_custom_call" | custom-call | flops 2621440 | bytes 6553600 | tf_op jit(solution)/shard_map/last/pallas_call | solution.py:430
Async XLA Ops:
  0.7 1.3 %copy-start = (bf16[640,1024]{1,0:T(8,128)(2,1)S(1)}, bf16[640,1024]{1,0:T(8,128)(2,1)}, u32[]{:S(2)}) copy-start(bf16[640,1024]{1,0:T(8,128)(2,1)} %x_ref.5) | copy-start | bytes 3932164
  2.0 1.0 copy-start.4
  3.0 0.9 copy-start.5
  3.9 0.7 copy-start.6
  4.6 0.7 copy-start.8
  5.3 3.8 %copy-start.7 = (f32[3,640]{1,0:T(4,128)S(1)}, f32[3,640]{1,0:T(4,128)}, u32[]{:S(2)}) copy-start(f32[3,640]{1,0:T(4,128)} %gain_ref.3) | copy-start | bytes 23044
  5.3 3.8 %copy-start.9 = (f32[3,640]{1,0:T(4,128)S(1)}, f32[3,640]{1,0:T(4,128)}, u32[]{:S(2)}) copy-start(f32[3,640]{1,0:T(4,128)} %bias_ref.3) | copy-start | bytes 23044
  8.6 27.0 %collective-permute-start.1 = (f32[1,640]{1,0:T(1,128)S(1)}, f32[1,640]{1,0:T(1,128)S(1)}, u32[]{:S(2)}, u32[]{:S(2)}) collective-permute-start(f32[1,640]{1,0:T(1,128)S(1)} %get-tuple-element.15.tv_ref), channel_id=1, source_target_pairs={{0,1},{1,0},{2,3},{3,2},{4,5},{5,4},{6,7},{7,6},{8,9},{9,8},{10,11... | collective-permute-start | bytes 7688 | tf_op jit(solution)/shard_map/ppermute | solution.py:323
  9.1 26.5 %collective-permute-start = (bf16[1024,640]{1,0:T(8,128)(2,1)}, bf16[1024,640]{1,0:T(8,128)(2,1)}, u32[]{:S(2)}, u32[]{:S(2)}) collective-permute-start(bf16[1024,640]{1,0:T(8,128)(2,1)} %get-tuple-element.14.own_ref), channel_id=1, source_target_pairs={{0,1},{1,0},{2,3},{3,2},{4,5},{5,4},{6,7},{7,6},{8,9},{9,8},{10,11... | collective-permute-start | bytes 3932168 | tf_op jit(solution)/shard_map/ppermute | solution.py:322
  9.1 1.3 %copy-start.11 = (bf16[640,1024]{1,0:T(8,128)(2,1)S(1)}, bf16[640,1024]{1,0:T(8,128)(2,1)}, u32[]{:S(2)}) copy-start(bf16[640,1024]{1,0:T(8,128)(2,1)} %x_ref.4) | copy-start | bytes 3932164
  10.4 25.1 %copy-start.10 = (bf16[640,1280]{1,0:T(8,128)(2,1)S(1)}, bf16[640,1280]{1,0:T(8,128)(2,1)}, u32[]{:S(2)}) copy-start(bf16[640,1280]{1,0:T(8,128)(2,1)} %ut_ref.1) | copy-start | bytes 4915204
  33.2 1.5 %copy-start.13 = (f32[1024,640]{1,0:T(8,128)}, f32[1024,640]{1,0:T(8,128)S(1)}, u32[]{:S(2)}) copy-start(f32[1024,640]{1,0:T(8,128)S(1)} %get-tuple-element.17.near_ref) | copy-start | bytes 7864324
  34.7 49.7 %collective-permute-start.2 = (bf16[1024,640]{1,0:T(8,128)(2,1)}, bf16[1024,640]{1,0:T(8,128)(2,1)}, u32[]{:S(2)}, u32[]{:S(2)}) collective-permute-start(bf16[1024,640]{1,0:T(8,128)(2,1)} %get-tuple-element.18), channel_id=1, source_target_pairs={{0,1},{1,0},{2,3},{3,2},{4,5},{5,4},{6,7},{7,6},{8,9},{9,8},{10,11... | collective-permute-start | bytes 3932168 | tf_op jit(solution)/shard_map/ppermute | solution.py:347
  35.6 48.8 %copy-start.3 = (bf16[640,1280]{1,0:T(8,128)(2,1)S(1)}, bf16[640,1280]{1,0:T(8,128)(2,1)}, u32[]{:S(2)}) copy-start(bf16[640,1280]{1,0:T(8,128)(2,1)} %z_ref.3) | copy-start | bytes 4915204
  35.6 48.8 %copy-start.12 = (s32[1,8,8]{2,1,0:T(8,128)S(1)}, s32[1,8,8]{2,1,0:T(8,128)}, u32[]{:S(2)}) copy-start(s32[1,8,8]{2,1,0:T(8,128)} %param.16) | copy-start | bytes 772
  35.6 48.8 %copy-start.14 = (f32[1024,640]{1,0:T(8,128)S(1)}, f32[1024,640]{1,0:T(8,128)}, u32[]{:S(2)}) copy-start(f32[1024,640]{1,0:T(8,128)} %copy-done.13) | copy-start | bytes 7864324
  84.4 2.2 %copy-start.2 = (bf16[1088,1920]{1,0:T(8,128)(2,1)S(1)}, bf16[1088,1920]{1,0:T(8,128)(2,1)}, u32[]{:S(2)}) copy-start(bf16[1088,1920]{1,0:T(8,128)(2,1)} %get-tuple-element.16.sh_ref) | copy-start | bytes 12533764
  100.6 9.3 %collective-permute-start.3 = (bf16[1024,640]{1,0:T(8,128)(2,1)S(1)}, bf16[1024,640]{1,0:T(8,128)(2,1)S(1)}, u32[]{:S(2)}, u32[]{:S(2)}) collective-permute-start(bf16[1024,640]{1,0:T(8,128)(2,1)S(1)} %get-tuple-element.22), channel_id=1, source_target_pairs={{0,1},{1,0},{2,3},{3,2},{4,5},{5,4},{6,7},{7,6},{8,9},{9,8},{10,11... | collective-permute-start | bytes 3932168 | tf_op jit(solution)/shard_map/ppermute | solution.py:408
  100.7 9.3 %copy-start.1 = (bf16[640,1024]{1,0:T(8,128)(2,1)S(1)}, bf16[640,1024]{1,0:T(8,128)(2,1)}, u32[]{:S(2)}) copy-start(bf16[640,1024]{1,0:T(8,128)(2,1)} %x_ref.5) | copy-start | bytes 3932164

commit v2 on v0

--- a/solution.py
+++ b/solution.py
@@ -1,8 +1,12 @@
+import functools
 import math
 
 import jax
 import jax.numpy as jnp
+import numpy as np
 from jax import lax
+from jax.experimental import pallas as pl
+from jax.experimental.pallas import tpu as pltpu
 from jax.sharding import PartitionSpec as P
 
 C = 1280
@@ -12,12 +16,550 @@
 TILE = 4
 VIEWS = 1
 
+BF = jnp.bfloat16
+F32 = jnp.float32
+WIDE = 256
+LANES = 128
+CHUNK = 2 * S
+FRONT_MIB = 32
+COVER_MIB = 24
+MIDDLE_MIB = 52
+LAST_MIB = 16
+
 
 def timestep_features(timestep):
     half_width = FREQ // 2
     rates = jnp.exp(-math.log(10000.0) * jnp.arange(half_width, dtype=jnp.float32) / half_width)
     angles = timestep.astype(jnp.float32)[0] * rates
     return jnp.concatenate([jnp.cos(angles), jnp.sin(angles)])
+
+
+NT = (((1,), (1,)), ((), ()))
+
+
+def half_silu(v):
+    h = 0.5 * v
+    return h + h * jnp.tanh(h)
+
+
+def group_masks(channels, size):
+    groups = channels // size
+    row = lax.broadcasted_iota(jnp.int32, (groups, channels), 0)
+    col = lax.broadcasted_iota(jnp.int32, (groups, channels), 1)
+    return ((col >= row * size) & (col < row * size + size)).astype(F32)
+
+
+def group_mean(sums, mask, count):
+    per_group = jnp.sum(mask * sums, axis=1, keepdims=True) * (1.0 / count)
+    return jnp.sum(mask * per_group, axis=0, keepdims=True)
+
+
+def each_chunk(cells, body, carry):
+    return lax.fori_loop(0, cells // CHUNK, lambda i, c: body(pl.multiple_of(i * CHUNK, CHUNK), c), carry)
+
+
+def norm_rows(xt, size, gain):
+    cells, channels = xt.shape
+    mask = group_masks(channels, size)
+
+    def fold(value):
+        return jnp.sum(value.reshape(CHUNK // 8, 8, channels), axis=0)
+
+    def add(start, total):
+        return total + fold(xt[pl.ds(start, CHUNK), :].astype(F32))
+
+    total = each_chunk(cells, add, jnp.zeros((8, channels), F32))
+    mean = group_mean(jnp.sum(total, axis=0, keepdims=True), mask, cells * size)
+
+    def add_square(start, total):
+        d = xt[pl.ds(start, CHUNK), :].astype(F32) - mean
+        return total + fold(d * d)
+
+    total = each_chunk(cells, add_square, jnp.zeros((8, channels), F32))
+    variance = group_mean(jnp.sum(total, axis=0, keepdims=True), mask, cells * size)
+    return mean, lax.rsqrt(variance + 1e-05) * gain
+
+
+def turn_in(x_ref, xt):
+    channels = x_ref.shape[0]
+    for b in range(channels // LANES):
+        part = slice(b * LANES, (b + 1) * LANES)
+        xt[:, part] = x_ref[part, :].T
+
+
+def edge_masks(rows, channels):
+    col = lax.broadcasted_iota(jnp.int32, (rows, channels), 0) % S
+    return col != 0, col != S - 1
+
+
+def activate(xt, sh, mean, scale, bias):
+    cells, channels = xt.shape
+    left_ok, right_ok = edge_masks(CHUNK, channels)
+
+    def body(start, _):
+        y = half_silu((xt[pl.ds(start, CHUNK), :].astype(F32) - mean) * scale + bias)
+        lo = jnp.where(left_ok, pltpu.roll(y, 1, 0), 0.0)
+        hi = jnp.where(right_ok, pltpu.roll(y, CHUNK - 1, 0), 0.0)
+        for k, v in enumerate((lo, y, hi)):
+            sh[pl.ds(start + S, CHUNK), k * channels:(k + 1) * channels] = v.astype(BF)
+        return 0
+
+    each_chunk(cells, body, 0)
+
+
+def clear_border(sh):
+    blank = jnp.zeros((S, sh.shape[1]), sh.dtype)
+    sh[0:S, :] = blank
+    sh[sh.shape[0] - S:, :] = blank
+
+
+def split3(row):
+    hi = row.astype(BF)
+    rest = row - hi.astype(F32)
+    mid = rest.astype(BF)
+    low = (rest - mid.astype(F32)).astype(BF)
+    place = lax.broadcasted_iota(jnp.int32, (8, row.shape[1]), 0)
+    parts = jnp.where(place == 0, hi.astype(F32), jnp.where(place == 1, mid.astype(F32), low.astype(F32)))
+    return jnp.where(place < 3, parts, 0.0).astype(BF)
+
+
+def conv_tile(sh, w, extra=None, z=None):
+    cells = sh.shape[0] - 2 * S
+    lhs = [sh[S * dy:S * dy + cells, :] for dy in range(3)]
+    rhs = w.reshape(w.shape[0] * w.shape[1], w.shape[2])
+    if extra is not None:
+        lhs.append(extra)
+        rhs = jnp.concatenate([rhs, z], axis=0)
+    return jnp.dot(jnp.concatenate(lhs, axis=1), rhs, preferred_element_type=F32)
+
+
+def keep_far(j, tiles, product, me, far, mixed):
+    far[:, columns_of(j)] = product.astype(BF)
+
+    @pl.when((j == 0) & (me == 0))
+    def _():
+        mixed[...] = product[:, :LANES]
+
+    @pl.when((j == tiles - 1) & (me == 1))
+    def _():
+        mixed[...] = product[:, LANES:]
+
+
+def columns_of(tile):
+    return pl.ds(pl.multiple_of(tile * WIDE, WIDE), WIDE)
+
+
+def far_columns(me, channels):
+    return pl.ds(pl.multiple_of((1 - me) * LANES, LANES), channels)
+
+
+def stage_front(me_ref, step_ref, x_hbm, h_hbm, gain_hbm, bias_hbm, rate_hbm, tw_hbm, w_hbm,
+                first_hbm, tv_hbm, far_hbm, mixed_hbm, ht_hbm, sh,
+                xv, hv, xt, ht, gain, bias, rate, tw, w, first, tv, far, mixed, sems, *, size, tiles):
+    channels, cells = hv.shape
+    me = me_ref[0]
+    far_tiles = -(-channels // WIDE)
+    start_tile = (1 - me) * (tiles - far_tiles)
+
+    def bring(src, dst, k):
+        c = pltpu.make_async_copy(src, dst, sems.at[k])
+        c.start()
+        return c
+
+    def weights(j):
+        return pltpu.make_async_copy(w_hbm.at[:, :, columns_of(start_tile + j)], w.at[j], sems.at[8 + j])
+
+    c_h = bring(h_hbm, hv, 0)
+    c_g = bring(gain_hbm, gain, 1)
+    c_b = bring(bias_hbm, bias, 2)
+    c_x = bring(x_hbm, xv, 3)
+    c_r = bring(rate_hbm, rate, 4)
+    c_t = bring(tw_hbm, tw, 5)
+    for j in range(far_tiles):
+        weights(j).start()
+    clear_border(sh)
+    c_h.wait()
+    turn_in(hv, ht)
+    out_ht = bring(ht, ht_hbm, 6)
+    c_g.wait()
+    c_b.wait()
+    mean, scale = norm_rows(ht, size, gain[2:3, :])
+    activate(ht, sh, mean, scale, bias[2:3, :])
+    c_x.wait()
+    c_r.wait()
+    c_t.wait()
+
+    turn_in(xv, xt)
+    mean, scale = norm_rows(xt, size, gain[0:1, :])
+    shift = bias[0:1, :]
+
+    def body(start, _):
+        y = half_silu((xt[pl.ds(start, CHUNK), :].astype(F32) - mean) * scale + shift)
+        first[pl.ds(start, CHUNK), :] = y.astype(BF)
+        return 0
+
+    each_chunk(cells, body, 0)
+    out_first = bring(first, first_hbm, 0)
+    angle = step_ref[0].astype(F32) * rate[...]
+    row = lax.broadcasted_iota(jnp.int32, angle.shape, 0)
+    features = jnp.where(row < angle.shape[0] // 2, jnp.cos(angle), jnp.sin(angle))
+    total = jnp.sum(tw[...].astype(F32) * features, axis=0, keepdims=True)
+    tv[...] = total / (1.0 + jnp.exp(-total))
+    out_tv = bring(tv, tv_hbm, 7)
+
+    def tile(j, _):
+        weights(j).wait()
+        keep_far(j, far_tiles, conv_tile(sh, w[j]), me, far, mixed)
+        return 0
+
+    lax.fori_loop(0, far_tiles, tile, 0)
+    out_far = bring(far.at[:, far_columns(me, channels)], far_hbm, 1)
+    out_mixed = bring(mixed, mixed_hbm, 2)
+    for c in (out_ht, out_tv, out_first, out_far, out_mixed):
+        c.wait()
+
+
+def stage_cover(me_ref, sh, w_hbm, near_hbm, w, near, sems, *, tiles):
+    channels = w_hbm.shape[1]
+    me = me_ref[0]
+    far_tiles = -(-channels // WIDE)
+    near_tiles = tiles - far_tiles
+
+    def weights(j):
+        return pltpu.make_async_copy(w_hbm.at[:, :, columns_of(me * far_tiles + j)], w.at[j], sems.at[j])
+
+    def result(j):
+        return pltpu.make_async_copy(
+            near.at[:, columns_of(j)], near_hbm.at[:, columns_of(j)], sems.at[near_tiles + j])
+
+    for j in range(near_tiles):
+        weights(j).start()
+
+    def tile(j, _):
+        weights(j).wait()
+        near[:, columns_of(j)] = conv_tile(sh, w[j])
+        result(j).start()
+        return 0
+
+    lax.fori_loop(0, near_tiles, tile, 0)
+    for j in range(near_tiles):
+        result(j).wait()
+
+
+def stage_middle(me_ref, mask_ref, own_hbm, got_hbm, tv_hbm, tvgot_hbm, gain_hbm, bias_hbm, ut_hbm, ct_hbm, win_hbm,
+                 wout_hbm, z_hbm, near_hbm, mixed_hbm, ht_hbm, cgot_hbm,
+                 far_hbm, mix_hbm, sh, state,
+                 xs, acc, xt, tv, tvgot, gain, bias, ut, ct, win, wout, z, near, ht, cgot, far, mix, sems,
+                 *, size, tiles):
+    cells, channels = xt.shape
+    full = xs.shape[1]
+    me = me_ref[0]
+    far_tiles = -(-channels // WIDE)
+    near_wide = near_hbm.shape[1]
+    start_tile = (1 - me) * (tiles - far_tiles)
+    mine = pl.ds(pl.multiple_of(me * channels, LANES), channels)
+    theirs = pl.ds(pl.multiple_of((1 - me) * channels, LANES), channels)
+    places = (1, 0, 2)
+
+    count = [0]
+
+    def bring(src, dst):
+        c = pltpu.make_async_copy(src, dst, sems.at[count[0]])
+        count[0] += 1
+        c.start()
+        return c
+
+    c_x = [bring(own_hbm, xs.at[pl.ds(S, cells), mine]), bring(got_hbm, xs.at[pl.ds(S, cells), theirs])]
+    c_in = [bring(win_hbm.at[:, places[0]], win.at[0])]
+    small = [bring(a, b) for a, b in ((tv_hbm, tv), (tvgot_hbm, tvgot), (gain_hbm, gain), (bias_hbm, bias),
+                                      (ut_hbm, ut), (ct_hbm, ct))]
+    clear_border(xs)
+    clear_border(sh)
+    c_in.append(bring(win_hbm.at[:, places[1]], win.at[1]))
+    side = [
+        bring(near_hbm, near.at[:, pl.ds(pl.multiple_of(me * LANES, LANES), near_wide)]),
+        bring(mixed_hbm, near.at[:, pl.ds(pl.multiple_of((1 - me) * near_wide, LANES), LANES)]),
+        bring(ht_hbm, ht),
+        bring(cgot_hbm, cgot),
+    ]
+    base = 17
+
+    def out_weights(j):
+        at = columns_of(start_tile + j)
+        return (
+            pltpu.make_async_copy(wout_hbm.at[:, :, at], wout.at[j], sems.at[base + 2 * j]),
+            pltpu.make_async_copy(z_hbm.at[:, at], z.at[j], sems.at[base + 2 * j + 1]),
+        )
+
+    for j in range(far_tiles):
+        for c in out_weights(j):
+            c.start()
+    for c in c_x + small:
+        c.wait()
+
+    def time_row(t_ref):
+        a = lax.dot_general(split3(tv[...]), t_ref[:, mine], NT, preferred_element_type=F32)
+        a = a + lax.dot_general(split3(tvgot[...]), t_ref[:, theirs], NT, preferred_element_type=F32)
+        return jnp.sum(a, axis=0, keepdims=True)
+
+    band = TILE * S
+    where = lax.broadcasted_iota(jnp.int32, (band, LANES), 0) % S // TILE
+
+    def gated_band(i, control_shift):
+        rows = slice(i * band, (i + 1) * band)
+        gate = jnp.zeros((band, LANES), F32)
+        for t in range(S // TILE):
+            gate = jnp.where(where == t, mask_ref[i, t].astype(F32), gate)
+        for b in range(channels // LANES):
+            part = slice(b * LANES, (b + 1) * LANES)
+            value = near[rows, part] + cgot[rows, part].astype(F32) + ht[rows, part].astype(F32)
+            value = (value + control_shift[:, part]).astype(BF).astype(F32)
+            state[rows, part] = (value * gate).astype(BF)
+
+    bands = cells // band
+    blocks = cells // WIDE
+    col = lax.broadcasted_iota(jnp.int32, (channels, WIDE), 1) % S
+    for s, place in enumerate(places):
+        c_in[s].wait()
+        if s == 1:
+            for c in side:
+                c.wait()
+            control_shift = time_row(ct)
+        weights = jnp.concatenate([win[s % 2, k] for k in range(3)], axis=1)
+        for cb in range(blocks):
+            rhs = jnp.concatenate([xs[S * dy + cb * WIDE:S * dy + cb * WIDE + WIDE, :] for dy in range(3)], axis=1)
+            p = lax.dot_general(weights, rhs, NT, preferred_element_type=F32)
+            part = slice(cb * WIDE, (cb + 1) * WIDE)
+            if place == 1:
+                acc[:, part] = p
+            elif place == 0:
+                acc[:, part] += jnp.where(col != 0, pltpu.roll(p, 1, 1), 0.0)
+            else:
+                acc[:, part] += jnp.where(col != S - 1, pltpu.roll(p, WIDE - 1, 1), 0.0)
+            if s == 1:
+                for i in range(cb * bands // blocks, (cb + 1) * bands // blocks):
+                    gated_band(i, control_shift)
+        if s == 0:
+            c_in.append(bring(win_hbm.at[:, places[2]], win.at[0]))
+
+    unet_shift = time_row(ut)
+    for b in range(channels // LANES):
+        part = slice(b * LANES, (b + 1) * LANES)
+        xt[:, part] = (acc[part, :].T + unet_shift[:, part]).astype(BF)
+    mean, scale = norm_rows(xt, size, gain[1:2, :])
+    activate(xt, sh, mean, scale, bias[1:2, :])
+
+    def tile(j, _):
+        for c in out_weights(j):
+            c.wait()
+        keep_far(j, far_tiles, conv_tile(sh, wout[j], state[...], z[j]), me, far, mix)
+        return 0
+
+    lax.fori_loop(0, far_tiles, tile, 0)
+    last = [bring(far.at[:, far_columns(me, channels)], far_hbm), bring(mix, mix_hbm)]
+    for c in last:
+        c.wait()
+
+
+def stage_near(me_ref, sh, state, w_hbm, z_hbm, near_hbm, w, z, near, sems, *, tiles):
+    channels = w_hbm.shape[1]
+    me = me_ref[0]
+    far_tiles = -(-channels // WIDE)
+    near_tiles = tiles - far_tiles
+
+    def weights(j):
+        at = columns_of(me * far_tiles + j)
+        return (
+            pltpu.make_async_copy(w_hbm.at[:, :, at], w.at[j], sems.at[2 * j]),
+            pltpu.make_async_copy(z_hbm.at[:, at], z.at[j], sems.at[2 * j + 1]),
+        )
+
+    def result(j):
+        return pltpu.make_async_copy(
+            near.at[:, columns_of(j)], near_hbm.at[:, columns_of(j)], sems.at[2 * near_tiles + j])
+
+    for j in range(near_tiles):
+        for c in weights(j):
+            c.start()
+
+    def tile(j, _):
+        for c in weights(j):
+            c.wait()
+        near[:, columns_of(j)] = conv_tile(sh, w[j], state[...], z[j])
+        result(j).start()
+        return 0
+
+    lax.fori_loop(0, near_tiles, tile, 0)
+    for j in range(near_tiles):
+        result(j).wait()
+
+
+def stage_last(me_ref, x_ref, near_ref, mixed_ref, got_ref, o_ref):
+    b = pl.program_id(0)
+    is_mixed = b == jnp.where(me_ref[0] == 0, pl.num_programs(0) - 1, 0)
+    local = jnp.where(is_mixed, mixed_ref[...], near_ref[...])
+    total = local + got_ref[...].astype(F32)
+    o_ref[...] = (x_ref[...].astype(F32) + total.T).astype(BF)
+
+
+def whole(shape):
+    return pl.BlockSpec(shape, lambda *_: (0,) * len(shape), pipeline_mode=pl.Buffered(1))
+
+
+def params(mib):
+    return pltpu.CompilerParams(vmem_limit_bytes=mib << 20)
+
+
+def far_off(*arrays):
+    return [pltpu.with_memory_space_constraint(a, pltpu.HBM) for a in arrays]
+
+
+def close(*arrays):
+    return [pltpu.with_memory_space_constraint(a, pltpu.VMEM) for a in arrays]
+
+
+def cost(flops, read):
+    return pl.CostEstimate(flops=flops, bytes_accessed=read, transcendentals=0)
+
+
+def local_pair(latent_x, control_h, tile_mask, timestep, time_weight, norm_gain, norm_bias, unet_conv_in,
+               unet_conv_out, control_conv, unet_temb, control_temb, zero_conv):
+    channels, cells = latent_x.shape
+    full = unet_conv_in.shape[2]
+    size = full // GROUPS
+    swap = [(0, 1), (1, 0)]
+    me = lax.axis_index("tensor").astype(jnp.int32).reshape(1)
+    half_width = FREQ // 2
+    rates = np.exp(-math.log(10000.0) * np.arange(half_width, dtype=np.float32) / half_width).astype(np.float32)
+    rates = jnp.asarray(np.concatenate([rates, rates])[:, None])
+    smem = pl.BlockSpec(memory_space=pltpu.SMEM)
+    anywhere = pl.BlockSpec(memory_space=pl.ANY)
+    vmem = pl.BlockSpec(memory_space=pltpu.VMEM)
+    dma = pltpu.SemaphoreType.DMA
+    tiles = full // WIDE
+    far_tiles = -(-channels // WIDE)
+    near_tiles = tiles - far_tiles
+    taps = control_conv.shape[0]
+    act = pltpu.HBM((cells, channels), BF)
+    padded = pltpu.VMEM((cells + 2 * S, 3 * channels), BF)
+    half_tile = pltpu.HBM((cells, LANES), F32)
+    near_out = pltpu.HBM((cells, near_tiles * WIDE), F32)
+    conv_flops = 2 * taps * channels * full * cells
+    conv_bytes = 2 * taps * channels * full
+
+    first, time_own, control_far, control_mixed, control_t, shifted = pl.pallas_call(
+        functools.partial(stage_front, size=size, tiles=tiles),
+        name="front",
+        out_shape=(act, pltpu.HBM((1, channels), F32), act, half_tile, act, padded),
+        in_specs=[smem, smem] + [anywhere] * 7,
+        out_specs=(anywhere,) * 5 + (vmem,),
+        scratch_shapes=[
+            pltpu.VMEM((channels, cells), BF),
+            pltpu.VMEM((channels, cells), BF),
+            pltpu.VMEM((cells, channels), BF),
+            pltpu.VMEM((cells, channels), BF),
+            pltpu.VMEM(norm_gain.shape, F32),
+            pltpu.VMEM(norm_bias.shape, F32),
+            pltpu.VMEM(rates.shape, F32),
+            pltpu.VMEM(time_weight.shape, BF),
+            pltpu.VMEM((far_tiles, taps, channels, WIDE), BF),
+            pltpu.VMEM((cells, channels), BF),
+            pltpu.VMEM((1, channels), F32),
+            pltpu.VMEM((cells, far_tiles * WIDE), BF),
+            pltpu.VMEM((cells, LANES), F32),
+            dma((8 + far_tiles,)),
+        ],
+        compiler_params=params(FRONT_MIB),
+        cost_estimate=cost(conv_flops * far_tiles // tiles, conv_bytes * far_tiles // tiles),
+    )(me, timestep, *far_off(latent_x, control_h, norm_gain, norm_bias, rates, time_weight, control_conv))
+    first_got = lax.ppermute(first, "tensor", swap)
+    time_got = lax.ppermute(time_own, "tensor", swap)
+    control_got = lax.ppermute(control_far, "tensor", swap)
+
+    control_near = pl.pallas_call(
+        functools.partial(stage_cover, tiles=tiles),
+        name="cover",
+        out_shape=near_out,
+        in_specs=[smem, vmem, anywhere],
+        out_specs=anywhere,
+        scratch_shapes=[
+            pltpu.VMEM((near_tiles, taps, channels, WIDE), BF),
+            pltpu.VMEM(near_out.shape, F32),
+            dma((2 * near_tiles,)),
+        ],
+        compiler_params=params(COVER_MIB),
+        cost_estimate=cost(conv_flops * near_tiles // tiles, conv_bytes * near_tiles // tiles),
+    )(me, *close(shifted), *far_off(control_conv))
+
+    mask = tile_mask.reshape(tile_mask.shape[1:])
+    far, mixed, second, state = pl.pallas_call(
+        functools.partial(stage_middle, size=size, tiles=tiles),
+        name="middle",
+        out_shape=(act, half_tile, padded, pltpu.VMEM((cells, channels), BF)),
+        in_specs=[smem, smem] + [anywhere] * 15,
+        out_specs=(anywhere, anywhere, vmem, vmem),
+        scratch_shapes=[
+            pltpu.VMEM((cells + 2 * S, full), BF),
+            pltpu.VMEM((channels, cells), F32),
+            pltpu.VMEM((cells, channels), BF),
+            pltpu.VMEM((1, channels), F32),
+            pltpu.VMEM((1, channels), F32),
+            pltpu.VMEM(norm_gain.shape, F32),
+            pltpu.VMEM(norm_bias.shape, F32),
+            pltpu.VMEM(unet_temb.shape, BF),
+            pltpu.VMEM(control_temb.shape, BF),
+            pltpu.VMEM((2, 3, channels, full), BF),
+            pltpu.VMEM((far_tiles, taps, channels, WIDE), BF),
+            pltpu.VMEM((far_tiles, channels, WIDE), BF),
+            pltpu.VMEM((cells, channels), F32),
+            pltpu.VMEM((cells, channels), BF),
+            pltpu.VMEM((cells, channels), BF),
+            pltpu.VMEM((cells, far_tiles * WIDE), BF),
+            pltpu.VMEM((cells, LANES), F32),
+            dma((17 + 2 * far_tiles,)),
+        ],
+        compiler_params=params(MIDDLE_MIB),
+        cost_estimate=cost(conv_flops * (tiles + far_tiles) // tiles, conv_bytes * (tiles + far_tiles) // tiles),
+    )(me, mask, *far_off(first, first_got, time_own, time_got, norm_gain, norm_bias, unet_temb, control_temb,
+                         unet_conv_in.reshape(3, 3, channels, full), unet_conv_out, zero_conv, control_near,
+                         control_mixed, control_t, control_got))
+    got = lax.ppermute(far, "tensor", swap)
+
+    near = pl.pallas_call(
+        functools.partial(stage_near, tiles=tiles),
+        name="near",
+        out_shape=near_out,
+        in_specs=[smem, vmem, vmem, anywhere, anywhere],
+        out_specs=anywhere,
+        scratch_shapes=[
+            pltpu.VMEM((near_tiles, taps, channels, WIDE), BF),
+            pltpu.VMEM((near_tiles, channels, WIDE), BF),
+            pltpu.VMEM(near_out.shape, F32),
+            dma((3 * near_tiles,)),
+        ],
+        compiler_params=params(COVER_MIB),
+        cost_estimate=cost(conv_flops * near_tiles // tiles, conv_bytes * near_tiles // tiles),
+    )(me, *close(second, state), *far_off(unet_conv_out, zero_conv))
+
+    last_near = near_tiles * WIDE // LANES - 1
+    return pl.pallas_call(
+        stage_last,
+        name="last",
+        out_shape=jax.ShapeDtypeStruct((channels, cells), BF),
+        grid_spec=pltpu.PrefetchScalarGridSpec(
+            num_scalar_prefetch=1,
+            grid=(channels // LANES,),
+            in_specs=[
+                pl.BlockSpec((LANES, cells), lambda b, i: (b, 0)),
+                pl.BlockSpec((cells, LANES), lambda b, i: (0, jnp.clip(b - i[0], 0, last_near))),
+                whole((cells, LANES)),
+                pl.BlockSpec((cells, LANES), lambda b, i: (0, b)),
+            ],
+            out_specs=pl.BlockSpec((LANES, cells), lambda b, i: (b, 0)),
+        ),
+        compiler_params=params(LAST_MIB),
+        cost_estimate=cost(4 * channels * cells, 10 * channels * cells),
+    )(me, latent_x, near, mixed, got)
 
 
 def norm_silu(inputs, scales, shifts):
@@ -71,7 +613,7 @@
     return spread_mask.reshape(VIEWS * S * S)
 
 
-def local(
+def local_any(
     latent_x,
     control_h,
     tile_mask,
@@ -150,6 +692,12 @@
         P("tensor", None),
         P("tensor", None),
     )
+
+    def local(latent_x, *rest):
+        channels, cells = latent_x.shape
+        paired = mesh.shape["tensor"] == 2 and channels % WIDE == LANES and VIEWS == 1 and cells == S * S
+        return (local_pair if paired else local_any)(latent_x, *rest)
+
     return jax.shard_map(
         local, mesh=mesh, in_specs=placed, out_specs=P("tensor", "dp"), check_vma=False
     )

time: 247 us -> 83.9 us (0.34); the launches traced: 244 us -> 83.6 us
  matrix products: 181 us -> 0 us
  Pallas kernels: 0 us -> 78.6 us
  local copies, waits for them, and re-layouts: 23.4 us -> 3.07 us
  waiting for transfers between devices: 13.8 us -> 0.01 us
  between operations: 14.4 us -> 0.77 us
  other arithmetic: 8.88 us -> 0 us
    dot_general x31 -> x0, matrix products: 181 us -> none  [the longest x18 110 us: conv_flipped(): lax.dot_general(weights[place], inputs, (((0,), (0,)), ((), ())), preferr...]
    pallas_call x0 -> x5, Pallas kernels: none -> 78.6 us  [the longest x1 37.5 us: local_pair(): pl.pallas_call(functools.partial(stage_middle, size=size, tiles=tiles), n...]
    unnamed x51 -> x12, local copies, waits for them, and re-layouts: 19.2 us -> 3.07 us
    unnamed x5 -> x0, waiting for transfers between devices: 13.8 us -> none
    convert_element_type x7 -> x0, other arithmetic: 4.74 us -> none  [the longest x1 2.7 us: local(): return (latent_x.astype(jnp.float32) + combined).astype(jnp.bfloat16)]
    reduce_sum x12 -> x0, other arithmetic: 3.96 us -> none  [the longest x6 2.87 us: norm_silu(): variance = jnp.mean(centred * centred, axis=(1, 3), keepdims=True)]
  transfers between devices with their start and end apart: 3 -> 4, of which waited for: 1 -> 0; matrix products, arithmetic and copies ran while one was open for 71% -> 0% of each run, Pallas kernels for 0% -> 24%
where the time goes in v2:
time: 83.9 us; the launch traced here: 83.6 us
  Pallas kernels  78.6 us (94%)
  local copies, waits for them, and re-layouts  3.07 us (4%)
  starting transfers between devices  1.15 us (1%)
    pallas_call x1, Pallas kernels, local_pair(): pl.pallas_call(functools.partial(stage_middle, size=size, tiles=tiles), n...  37.5 us
    pallas_call x1, Pallas kernels, local_pair(): pl.pallas_call(functools.partial(stage_front, size=size, tiles=tiles), na...  18.2 us
    pallas_call x1, Pallas kernels, local_pair(): pl.pallas_call(functools.partial(stage_near, tiles=tiles), name='near', o...  10.2 us
    pallas_call x1, Pallas kernels, local_pair(): pl.pallas_call(functools.partial(stage_cover, tiles=tiles), name='cover',...  9.5 us
    pallas_call x1, Pallas kernels, local_pair(): pl.pallas_call(stage_last, name='last', out_shape=jax.ShapeDtypeStruct((c...  3.14 us
    unnamed x12, local copies, waits for them, and re-layouts  3.07 us
  transfers between devices with their start and end apart: 4, of which 0 were waited for; matrix products, arithmetic and copies ran while one was open for 0% of the time, Pallas kernels for 24%

profile of v2, /device:TPU:0, one launch (start us, length us, event | category | flops | bytes accessed | tf_op | source)
XLA Modules:
  0.0 83.6 jit_solution(4285571159397383662)
XLA Ops:
  0.7 18.2 %front.1 = (bf16[1024,640]{1,0:T(8,128)(2,1)}, f32[1,640]{1,0:T(1,128)}, bf16[1024,640]{1,0:T(8,128)(2,1)}, f32[1024,128]{1,0:T(8,128)}, bf16[1024,640]{1,0:T(8,128)(2,1)}, /*index=5*/bf16[1088,1920]{1,0:T(8,128)(2,1)S(1)}) custom-call(s32[1]{0:T(128)} %bitcast.me_ref, s32[1]{0:T(128)S(6)} %copy.15.step_ref, bf16[640,1024]{1,0:T(8,128)(2,1)} %x_ref.1, ...), custom_call_target="tpu_custom_call" | custom-call | flops 9059696640 | bytes 8847360 | tf_op jit(solution)/shard_map/front/pallas_call | solution.py:450
  18.9 0.5 collective-permute-start.2
  19.4 0.1 collective-permute-start
  19.5 0.4 collective-permute-start.1
  19.9 9.5 %cover.1.near_hbm = f32[1024,512]{1,0:T(8,128)} custom-call(s32[1]{0:T(128)} %bitcast.me_ref, bf16[1088,1920]{1,0:T(8,128)(2,1)S(1)} %get-tuple-element.17.sh, bf16[9,640,1280]{2,1,0:T(8,128)(2,1)} %w_hbm.4), custom_call_target="tpu_custom_call" | custom-call | flops 6039797760 | bytes 5898240 | tf_op jit(solution)/shard_map/cover/pallas_call | solution.py:479
  29.4 0.0 collective-permute-done.1.tvgot_hbm
  29.4 0.0 copy-start.5
  29.4 0.0 collective-permute-done.2.cgot_hbm
  29.4 0.0 copy-start.3
  29.5 0.0 collective-permute-done.got_hbm
  29.5 0.0 copy-start.4
  29.5 0.5 copy-done.5
  30.0 0.5 copy-done.3
  30.5 0.4 copy-done.4
  31.0 37.5 %middle.1 = (bf16[1024,640]{1,0:T(8,128)(2,1)}, f32[1024,128]{1,0:T(8,128)}, bf16[1088,1920]{1,0:T(8,128)(2,1)S(1)}, bf16[1024,640]{1,0:T(8,128)(2,1)S(1)}) custom-call(s32[1]{0:T(128)} %bitcast.me_ref, s32[8,8]{1,0:T(8,128)} %bitcast.4, bf16[1024,640]{1,0:T(8,128)(2,1)} %get-tuple-element.15.own_hbm, bf16[1024,640]{1,0:T(8,128)(2,1)} %copy-done.4, ...), custom_call_target="tpu_custom_call" | custom-call | flops 24159191040 | bytes 23592960 | tf_op jit(solution)/shard_map/middle/pallas_call | solution.py:495
  68.5 0.1 collective-permute-start.3
  68.6 0.0 copy-start.1
  68.6 0.0 copy-start.2
  68.6 10.2 %near.1.near_ref = f32[1024,512]{1,0:T(8,128)} custom-call(s32[1]{0:T(128)} %bitcast.me_ref, bf16[1088,1920]{1,0:T(8,128)(2,1)S(1)} %get-tuple-element.21.sh, bf16[1024,640]{1,0:T(8,128)(2,1)S(1)} %get-tuple-element.22.state, bf16[9,640,1280]{2,1,0:T(8,128)(2,1)} %w_hbm.5, bf16[640,1280]{1,0:T(8,128)(2,1)} %z_hbm.3), custom_call_target="tpu_custom_call" | custom-call | flops 6039797760 | bytes 5898240 | tf_op jit(solution)/shard_map/near/pallas_call | solution.py:528
  78.8 0.0 collective-permute-done.3.got_ref
  78.8 0.0 copy-done.1
  78.8 0.0 copy-done.2
  78.8 0.0 copy-start
  78.8 1.6 %copy-done = f32[1024,512]{1,0:T(8,128)S(1)} copy-done((f32[1024,512]{1,0:T(8,128)S(1)}, f32[1024,512]{1,0:T(8,128)}, u32[]{:S(2)}) %copy-start) | copy-done | bytes 2097176
  80.4 3.1 %last.1 = bf16[640,1024]{1,0:T(8,128)(2,1)} custom-call(s32[1]{0:T(128)} %bitcast.me_ref, bf16[640,1024]{1,0:T(8,128)(2,1)S(1)} %copy-done.1, f32[1024,512]{1,0:T(8,128)S(1)} %copy-done, f32[1024,128]{1,0:T(8,128)S(1)} %copy-done.2, bf16[1024,640]{1,0:T(8,128)(2,1)S(1)} %collective-permute-done.3.got_ref), custom_call_target="tpu_custom_call" | custom-call | flops 2621440 | bytes 6553600 | tf_op jit(solution)/shard_map/last/pallas_call | solution.py:545
Async XLA Ops:
  18.9 10.6 %collective-permute-start.2 = (bf16[1024,640]{1,0:T(8,128)(2,1)}, bf16[1024,640]{1,0:T(8,128)(2,1)S(1)}, u32[]{:S(2)}, u32[]{:S(2)}) collective-permute-start(bf16[1024,640]{1,0:T(8,128)(2,1)} %get-tuple-element.20), channel_id=1, source_target_pairs={{0,1},{1,0},{2,3},{3,2},{4,5},{5,4},{6,7},{7,6},{8,9},{9,8},{10,11... | collective-permute-start | bytes 3932168 | tf_op jit(solution)/shard_map/ppermute | solution.py:477
  19.4 10.1 %collective-permute-start = (bf16[1024,640]{1,0:T(8,128)(2,1)}, bf16[1024,640]{1,0:T(8,128)(2,1)S(1)}, u32[]{:S(2)}, u32[]{:S(2)}) collective-permute-start(bf16[1024,640]{1,0:T(8,128)(2,1)} %get-tuple-element.15.own_hbm), channel_id=1, source_target_pairs={{0,1},{1,0},{2,3},{3,2},{4,5},{5,4},{6,7},{7,6},{8,9},{9,8},{10,11... | collective-permute-start | bytes 3932168 | tf_op jit(solution)/shard_map/ppermute | solution.py:475
  19.5 9.9 %collective-permute-start.1 = (f32[1,640]{1,0:T(1,128)}, f32[1,640]{1,0:T(1,128)S(1)}, u32[]{:S(2)}, u32[]{:S(2)}) collective-permute-start(f32[1,640]{1,0:T(1,128)} %get-tuple-element.16.tv_hbm), channel_id=1, source_target_pairs={{0,1},{1,0},{2,3},{3,2},{4,5},{5,4},{6,7},{7,6},{8,9},{9,8},{10,11... | collective-permute-start | bytes 7688 | tf_op jit(solution)/shard_map/ppermute | solution.py:476
  29.4 0.6 copy-start.5
  29.4 1.1 %copy-start.3 = (bf16[1024,640]{1,0:T(8,128)(2,1)}, bf16[1024,640]{1,0:T(8,128)(2,1)S(1)}, u32[]{:S(2)}) copy-start(bf16[1024,640]{1,0:T(8,128)(2,1)S(1)} %collective-permute-done.2.cgot_hbm) | copy-start | bytes 3932164
  29.5 1.5 %copy-start.4 = (bf16[1024,640]{1,0:T(8,128)(2,1)}, bf16[1024,640]{1,0:T(8,128)(2,1)S(1)}, u32[]{:S(2)}) copy-start(bf16[1024,640]{1,0:T(8,128)(2,1)S(1)} %collective-permute-done.got_hbm) | copy-start | bytes 3932164
  68.5 10.3 %collective-permute-start.3 = (bf16[1024,640]{1,0:T(8,128)(2,1)}, bf16[1024,640]{1,0:T(8,128)(2,1)S(1)}, u32[]{:S(2)}, u32[]{:S(2)}) collective-permute-start(bf16[1024,640]{1,0:T(8,128)(2,1)} %get-tuple-element.24), channel_id=1, source_target_pairs={{0,1},{1,0},{2,3},{3,2},{4,5},{5,4},{6,7},{7,6},{8,9},{9,8},{10,11... | collective-permute-start | bytes 3932168 | tf_op jit(solution)/shard_map/ppermute | solution.py:526
  68.6 10.2 %copy-start.1 = (bf16[640,1024]{1,0:T(8,128)(2,1)S(1)}, bf16[640,1024]{1,0:T(8,128)(2,1)}, u32[]{:S(2)}) copy-start(bf16[640,1024]{1,0:T(8,128)(2,1)} %x_ref.1) | copy-start | bytes 3932164
  68.6 10.2 %copy-start.2 = (f32[1024,128]{1,0:T(8,128)S(1)}, f32[1024,128]{1,0:T(8,128)}, u32[]{:S(2)}) copy-start(f32[1024,128]{1,0:T(8,128)} %get-tuple-element.23.mixed_ref) | copy-start | bytes 1572868
  78.8 1.6 %copy-start = (f32[1024,512]{1,0:T(8,128)S(1)}, f32[1024,512]{1,0:T(8,128)}, u32[]{:S(2)}) copy-start(f32[1024,512]{1,0:T(8,128)} %near.1.near_ref) | copy-start | bytes 6291460

commit v3 on v2

--- a/solution.py
+++ b/solution.py
@@ -21,9 +21,10 @@
 WIDE = 256
 LANES = 128
 CHUNK = 2 * S
+NORM = 8 * S
 FRONT_MIB = 32
 COVER_MIB = 24
-MIDDLE_MIB = 52
+MIDDLE_MIB = 48
 LAST_MIB = 16
 
 
@@ -37,8 +38,7 @@
 NT = (((1,), (1,)), ((), ()))
 
 
-def half_silu(v):
-    h = 0.5 * v
+def silu_of_half(h):
     return h + h * jnp.tanh(h)
 
 
@@ -54,8 +54,8 @@
     return jnp.sum(mask * per_group, axis=0, keepdims=True)
 
 
-def each_chunk(cells, body, carry):
-    return lax.fori_loop(0, cells // CHUNK, lambda i, c: body(pl.multiple_of(i * CHUNK, CHUNK), c), carry)
+def each_chunk(cells, body, carry, rows=CHUNK):
+    return lax.fori_loop(0, cells // rows, lambda i, c: body(pl.multiple_of(i * rows, rows), c), carry)
 
 
 def norm_rows(xt, size, gain):
@@ -63,21 +63,21 @@
     mask = group_masks(channels, size)
 
     def fold(value):
-        return jnp.sum(value.reshape(CHUNK // 8, 8, channels), axis=0)
+        return jnp.sum(value.reshape(NORM // 8, 8, channels), axis=0)
 
     def add(start, total):
-        return total + fold(xt[pl.ds(start, CHUNK), :].astype(F32))
-
-    total = each_chunk(cells, add, jnp.zeros((8, channels), F32))
+        return total + fold(xt[pl.ds(start, NORM), :].astype(F32))
+
+    total = each_chunk(cells, add, jnp.zeros((8, channels), F32), NORM)
     mean = group_mean(jnp.sum(total, axis=0, keepdims=True), mask, cells * size)
 
     def add_square(start, total):
-        d = xt[pl.ds(start, CHUNK), :].astype(F32) - mean
+        d = xt[pl.ds(start, NORM), :].astype(F32) - mean
         return total + fold(d * d)
 
-    total = each_chunk(cells, add_square, jnp.zeros((8, channels), F32))
+    total = each_chunk(cells, add_square, jnp.zeros((8, channels), F32), NORM)
     variance = group_mean(jnp.sum(total, axis=0, keepdims=True), mask, cells * size)
-    return mean, lax.rsqrt(variance + 1e-05) * gain
+    return mean, lax.rsqrt(variance + 1e-05) * (0.5 * gain)
 
 
 def turn_in(x_ref, xt):
@@ -94,10 +94,11 @@
 
 def activate(xt, sh, mean, scale, bias):
     cells, channels = xt.shape
+    bias = 0.5 * bias
     left_ok, right_ok = edge_masks(CHUNK, channels)
 
     def body(start, _):
-        y = half_silu((xt[pl.ds(start, CHUNK), :].astype(F32) - mean) * scale + bias)
+        y = silu_of_half((xt[pl.ds(start, CHUNK), :].astype(F32) - mean) * scale + bias)
         lo = jnp.where(left_ok, pltpu.roll(y, 1, 0), 0.0)
         hi = jnp.where(right_ok, pltpu.roll(y, CHUNK - 1, 0), 0.0)
         for k, v in enumerate((lo, y, hi)):
@@ -172,13 +173,13 @@
     c_h = bring(h_hbm, hv, 0)
     c_g = bring(gain_hbm, gain, 1)
     c_b = bring(bias_hbm, bias, 2)
+    clear_border(sh)
+    c_h.wait()
     c_x = bring(x_hbm, xv, 3)
     c_r = bring(rate_hbm, rate, 4)
     c_t = bring(tw_hbm, tw, 5)
     for j in range(far_tiles):
         weights(j).start()
-    clear_border(sh)
-    c_h.wait()
     turn_in(hv, ht)
     out_ht = bring(ht, ht_hbm, 6)
     c_g.wait()
@@ -191,19 +192,19 @@
 
     turn_in(xv, xt)
     mean, scale = norm_rows(xt, size, gain[0:1, :])
-    shift = bias[0:1, :]
+    shift = 0.5 * bias[0:1, :]
 
     def body(start, _):
-        y = half_silu((xt[pl.ds(start, CHUNK), :].astype(F32) - mean) * scale + shift)
+        y = silu_of_half((xt[pl.ds(start, CHUNK), :].astype(F32) - mean) * scale + shift)
         first[pl.ds(start, CHUNK), :] = y.astype(BF)
         return 0
 
     each_chunk(cells, body, 0)
     out_first = bring(first, first_hbm, 0)
     angle = step_ref[0].astype(F32) * rate[...]
-    row = lax.broadcasted_iota(jnp.int32, angle.shape, 0)
-    features = jnp.where(row < angle.shape[0] // 2, jnp.cos(angle), jnp.sin(angle))
-    total = jnp.sum(tw[...].astype(F32) * features, axis=0, keepdims=True)
+    col = lax.broadcasted_iota(jnp.int32, angle.shape, 1)
+    features = jnp.where(col < angle.shape[1] // 2, jnp.cos(angle), jnp.sin(angle))
+    total = jnp.sum(jnp.dot(split3(features), tw[...], preferred_element_type=F32), axis=0, keepdims=True)
     tv[...] = total / (1.0 + jnp.exp(-total))
     out_tv = bring(tv, tv_hbm, 7)
 
@@ -232,11 +233,15 @@
         return pltpu.make_async_copy(
             near.at[:, columns_of(j)], near_hbm.at[:, columns_of(j)], sems.at[near_tiles + j])
 
-    for j in range(near_tiles):
-        weights(j).start()
+    weights(0).start()
 
     def tile(j, _):
         weights(j).wait()
+
+        @pl.when(j + 1 < near_tiles)
+        def _():
+            weights(j + 1).start()
+
         near[:, columns_of(j)] = conv_tile(sh, w[j])
         result(j).start()
         return 0
@@ -246,10 +251,10 @@
         result(j).wait()
 
 
-def stage_middle(me_ref, mask_ref, own_hbm, got_hbm, tv_hbm, tvgot_hbm, gain_hbm, bias_hbm, ut_hbm, ct_hbm, win_hbm,
-                 wout_hbm, z_hbm, near_hbm, mixed_hbm, ht_hbm, cgot_hbm,
+def stage_middle(me_ref, mask_ref, got_ref, tvgot, cgot, own_hbm, tv_hbm, gain_hbm, bias_hbm, ut_hbm, ct_hbm, win_hbm,
+                 wout_hbm, z_hbm, near_hbm, mixed_hbm, ht_hbm,
                  far_hbm, mix_hbm, sh, state,
-                 xs, acc, xt, tv, tvgot, gain, bias, ut, ct, win, wout, z, near, ht, cgot, far, mix, sems,
+                 xs, acc, xt, tv, gain, bias, ut, ct, win, wout, z, near, ht, far, mix, sems,
                  *, size, tiles):
     cells, channels = xt.shape
     full = xs.shape[1]
@@ -269,19 +274,11 @@
         c.start()
         return c
 
-    c_x = [bring(own_hbm, xs.at[pl.ds(S, cells), mine]), bring(got_hbm, xs.at[pl.ds(S, cells), theirs])]
+    c_x = [bring(own_hbm, xs.at[pl.ds(S, cells), mine])]
     c_in = [bring(win_hbm.at[:, places[0]], win.at[0])]
-    small = [bring(a, b) for a, b in ((tv_hbm, tv), (tvgot_hbm, tvgot), (gain_hbm, gain), (bias_hbm, bias),
-                                      (ut_hbm, ut), (ct_hbm, ct))]
     clear_border(xs)
     clear_border(sh)
-    c_in.append(bring(win_hbm.at[:, places[1]], win.at[1]))
-    side = [
-        bring(near_hbm, near.at[:, pl.ds(pl.multiple_of(me * LANES, LANES), near_wide)]),
-        bring(mixed_hbm, near.at[:, pl.ds(pl.multiple_of((1 - me) * near_wide, LANES), LANES)]),
-        bring(ht_hbm, ht),
-        bring(cgot_hbm, cgot),
-    ]
+    xs[S:S + cells, theirs] = got_ref[...]
     base = 17
 
     def out_weights(j):
@@ -291,11 +288,15 @@
             pltpu.make_async_copy(z_hbm.at[:, at], z.at[j], sems.at[base + 2 * j + 1]),
         )
 
-    for j in range(far_tiles):
-        for c in out_weights(j):
-            c.start()
-    for c in c_x + small:
-        c.wait()
+    c_x[0].wait()
+    c_in[0].wait()
+    small = [bring(a, b) for a, b in ((tv_hbm, tv), (gain_hbm, gain), (bias_hbm, bias), (ut_hbm, ut), (ct_hbm, ct))]
+    side = [
+        bring(near_hbm, near.at[:, pl.ds(pl.multiple_of(me * LANES, LANES), near_wide)]),
+        bring(mixed_hbm, near.at[:, pl.ds(pl.multiple_of((1 - me) * near_wide, LANES), LANES)]),
+        bring(ht_hbm, ht),
+    ]
+    c_in.append(bring(win_hbm.at[:, places[1]], win.at[1]))
 
     def time_row(t_ref):
         a = lax.dot_general(split3(tv[...]), t_ref[:, mine], NT, preferred_element_type=F32)
@@ -313,16 +314,16 @@
         for b in range(channels // LANES):
             part = slice(b * LANES, (b + 1) * LANES)
             value = near[rows, part] + cgot[rows, part].astype(F32) + ht[rows, part].astype(F32)
-            value = (value + control_shift[:, part]).astype(BF).astype(F32)
-            state[rows, part] = (value * gate).astype(BF)
+            state[rows, part] = ((value + control_shift[:, part]) * gate).astype(BF)
 
     bands = cells // band
     blocks = cells // WIDE
     col = lax.broadcasted_iota(jnp.int32, (channels, WIDE), 1) % S
     for s, place in enumerate(places):
-        c_in[s].wait()
+        if s > 0:
+            c_in[s].wait()
         if s == 1:
-            for c in side:
+            for c in small + side:
                 c.wait()
             control_shift = time_row(ct)
         weights = jnp.concatenate([win[s % 2, k] for k in range(3)], axis=1)
@@ -341,6 +342,9 @@
                     gated_band(i, control_shift)
         if s == 0:
             c_in.append(bring(win_hbm.at[:, places[2]], win.at[0]))
+            for j in range(far_tiles):
+                for c in out_weights(j):
+                    c.start()
 
     unet_shift = time_row(ut)
     for b in range(channels // LANES):
@@ -361,7 +365,7 @@
         c.wait()
 
 
-def stage_near(me_ref, sh, state, w_hbm, z_hbm, near_hbm, w, z, near, sems, *, tiles):
+def stage_near(me_ref, sh, state, w_hbm, z_hbm, near, w, z, sems, *, tiles):
     channels = w_hbm.shape[1]
     me = me_ref[0]
     far_tiles = -(-channels // WIDE)
@@ -374,24 +378,22 @@
             pltpu.make_async_copy(z_hbm.at[:, at], z.at[j], sems.at[2 * j + 1]),
         )
 
-    def result(j):
-        return pltpu.make_async_copy(
-            near.at[:, columns_of(j)], near_hbm.at[:, columns_of(j)], sems.at[2 * near_tiles + j])
-
-    for j in range(near_tiles):
-        for c in weights(j):
-            c.start()
+    for c in weights(0):
+        c.start()
 
     def tile(j, _):
         for c in weights(j):
             c.wait()
+
+        @pl.when(j + 1 < near_tiles)
+        def _():
+            for c in weights(j + 1):
+                c.start()
+
         near[:, columns_of(j)] = conv_tile(sh, w[j], state[...], z[j])
-        result(j).start()
         return 0
 
     lax.fori_loop(0, near_tiles, tile, 0)
-    for j in range(near_tiles):
-        result(j).wait()
 
 
 def stage_last(me_ref, x_ref, near_ref, mixed_ref, got_ref, o_ref):
@@ -431,7 +433,7 @@
     me = lax.axis_index("tensor").astype(jnp.int32).reshape(1)
     half_width = FREQ // 2
     rates = np.exp(-math.log(10000.0) * np.arange(half_width, dtype=np.float32) / half_width).astype(np.float32)
-    rates = jnp.asarray(np.concatenate([rates, rates])[:, None])
+    rates = jnp.asarray(np.concatenate([rates, rates])[None, :])
     smem = pl.BlockSpec(memory_space=pltpu.SMEM)
     anywhere = pl.BlockSpec(memory_space=pl.ANY)
     vmem = pl.BlockSpec(memory_space=pltpu.VMEM)
@@ -496,13 +498,12 @@
         functools.partial(stage_middle, size=size, tiles=tiles),
         name="middle",
         out_shape=(act, half_tile, padded, pltpu.VMEM((cells, channels), BF)),
-        in_specs=[smem, smem] + [anywhere] * 15,
+        in_specs=[smem, smem, vmem, vmem, vmem] + [anywhere] * 12,
         out_specs=(anywhere, anywhere, vmem, vmem),
         scratch_shapes=[
             pltpu.VMEM((cells + 2 * S, full), BF),
             pltpu.VMEM((channels, cells), F32),
             pltpu.VMEM((cells, channels), BF),
-            pltpu.VMEM((1, channels), F32),
             pltpu.VMEM((1, channels), F32),
             pltpu.VMEM(norm_gain.shape, F32),
             pltpu.VMEM(norm_bias.shape, F32),
@@ -513,29 +514,28 @@
             pltpu.VMEM((far_tiles, channels, WIDE), BF),
             pltpu.VMEM((cells, channels), F32),
             pltpu.VMEM((cells, channels), BF),
-            pltpu.VMEM((cells, channels), BF),
             pltpu.VMEM((cells, far_tiles * WIDE), BF),
             pltpu.VMEM((cells, LANES), F32),
             dma((17 + 2 * far_tiles,)),
         ],
         compiler_params=params(MIDDLE_MIB),
         cost_estimate=cost(conv_flops * (tiles + far_tiles) // tiles, conv_bytes * (tiles + far_tiles) // tiles),
-    )(me, mask, *far_off(first, first_got, time_own, time_got, norm_gain, norm_bias, unet_temb, control_temb,
-                         unet_conv_in.reshape(3, 3, channels, full), unet_conv_out, zero_conv, control_near,
-                         control_mixed, control_t, control_got))
+    )(me, mask, *close(first_got, time_got, control_got),
+      *far_off(first, time_own, norm_gain, norm_bias, unet_temb, control_temb,
+               unet_conv_in.reshape(3, 3, channels, full), unet_conv_out, zero_conv, control_near,
+               control_mixed, control_t))
     got = lax.ppermute(far, "tensor", swap)
 
     near = pl.pallas_call(
         functools.partial(stage_near, tiles=tiles),
         name="near",
-        out_shape=near_out,
+        out_shape=pltpu.VMEM(near_out.shape, F32),
         in_specs=[smem, vmem, vmem, anywhere, anywhere],
-        out_specs=anywhere,
+        out_specs=vmem,
         scratch_shapes=[
             pltpu.VMEM((near_tiles, taps, channels, WIDE), BF),
             pltpu.VMEM((near_tiles, channels, WIDE), BF),
-            pltpu.VMEM(near_out.shape, F32),
-            dma((3 * near_tiles,)),
+            dma((2 * near_tiles,)),
         ],
         compiler_params=params(COVER_MIB),
         cost_estimate=cost(conv_flops * near_tiles // tiles, conv_bytes * near_tiles // tiles),

time: 83.9 us -> 77.5 us (0.924)
  Pallas kernels: 78.6 us -> 75.2 us
  local copies, waits for them, and re-layouts: 3.07 us -> 0.01 us
    unnamed x12 -> x4, local copies, waits for them, and re-layouts: 3.07 us -> 0.01 us
    pallas_call x1, Pallas kernels: 37.5 us -> 35.9 us  [local_pair(): pl.pallas_call(functools.partial(stage_middle, size=size, tiles=tiles), n...]
    pallas_call x1, Pallas kernels: 10.2 us -> 9.15 us  [local_pair(): pl.pallas_call(functools.partial(stage_near, tiles=tiles), name='near', o...]
where the time goes in v3:
time: 77.5 us; the launch traced here: 77.1 us
  Pallas kernels  75.2 us (97%)
  starting transfers between devices  1.13 us (1%)
    pallas_call x1, Pallas kernels, local_pair(): pl.pallas_call(functools.partial(stage_middle, size=size, tiles=tiles), n...  35.9 us
    pallas_call x1, Pallas kernels, local_pair(): pl.pallas_call(functools.partial(stage_front, size=size, tiles=tiles), na...  17.5 us
    pallas_call x1, Pallas kernels, local_pair(): pl.pallas_call(functools.partial(stage_cover, tiles=tiles), name='cover',...  9.53 us
    pallas_call x1, Pallas kernels, local_pair(): pl.pallas_call(functools.partial(stage_near, tiles=tiles), name='near', o...  9.15 us
    pallas_call x1, Pallas kernels, local_pair(): pl.pallas_call(stage_last, name='last', out_shape=jax.ShapeDtypeStruct((c...  3.17 us
  transfers between devices with their start and end apart: 4, of which 0 were waited for; matrix products, arithmetic and copies ran while one was open for 0% of the time, Pallas kernels for 24%

profile of v3, /device:TPU:0, one launch (start us, length us, event | category | flops | bytes accessed | tf_op | source)
XLA Modules:
  0.0 77.1 jit_solution(3707378477956048809)
XLA Ops:
  0.7 17.5 %front.1 = (bf16[1024,640]{1,0:T(8,128)(2,1)}, f32[1,640]{1,0:T(1,128)}, bf16[1024,640]{1,0:T(8,128)(2,1)}, f32[1024,128]{1,0:T(8,128)}, bf16[1024,640]{1,0:T(8,128)(2,1)}, /*index=5*/bf16[1088,1920]{1,0:T(8,128)(2,1)S(1)}) custom-call(s32[1]{0:T(128)} %bitcast.me_ref, s32[1]{0:T(128)S(6)} %copy.15.step_ref, bf16[640,1024]{1,0:T(8,128)(2,1)} %x_ref.1, ...), custom_call_target="tpu_custom_call" | custom-call | flops 9059696640 | bytes 8847360 | tf_op jit(solution)/shard_map/front/pallas_call | solution.py:452
  18.1 0.5 collective-permute-start.2
  18.7 0.1 collective-permute-start
  18.7 0.4 collective-permute-start.1
  19.2 9.5 %cover.1.near_hbm = f32[1024,512]{1,0:T(8,128)} custom-call(s32[1]{0:T(128)} %bitcast.me_ref, bf16[1088,1920]{1,0:T(8,128)(2,1)S(1)} %get-tuple-element.18.sh, bf16[9,640,1280]{2,1,0:T(8,128)(2,1)} %w_hbm.4), custom_call_target="tpu_custom_call" | custom-call | flops 6039797760 | bytes 5898240 | tf_op jit(solution)/shard_map/cover/pallas_call | solution.py:481
  28.7 0.0 collective-permute-done.1.tvgot
  28.7 0.0 collective-permute-done.2.cgot
  28.7 0.0 collective-permute-done.got_ref
  28.7 35.9 %middle.1 = (bf16[1024,640]{1,0:T(8,128)(2,1)}, f32[1024,128]{1,0:T(8,128)}, bf16[1088,1920]{1,0:T(8,128)(2,1)S(1)}, bf16[1024,640]{1,0:T(8,128)(2,1)S(1)}) custom-call(s32[1]{0:T(128)} %bitcast.me_ref, s32[8,8]{1,0:T(8,128)} %bitcast.4, bf16[1024,640]{1,0:T(8,128)(2,1)S(1)} %collective-permute-done.got_ref, f32[1,640]{1,0:T(1,128)S(1)} %collective-permute-done.1.tvgot, ...), custom_call_target="tpu_custom_call" | custom-call | flops 24159191040 | bytes 23592960 | tf_op jit(solution)/shard_map/middle/pallas_call | solution.py:497
  64.6 0.1 collective-permute-start.3
  64.7 0.0 copy-start
  64.7 0.0 copy-start.1
  64.7 9.2 %near.1.near_ref = f32[1024,512]{1,0:T(8,128)S(1)} custom-call(s32[1]{0:T(128)} %bitcast.me_ref, bf16[1088,1920]{1,0:T(8,128)(2,1)S(1)} %get-tuple-element.21.sh, bf16[1024,640]{1,0:T(8,128)(2,1)S(1)} %get-tuple-element.22.state, bf16[9,640,1280]{2,1,0:T(8,128)(2,1)} %w_hbm.5, bf16[640,1280]{1,0:T(8,128)(2,1)} %z_hbm.3), custom_call_target="tpu_custom_call" | custom-call | flops 6039797760 | bytes 5898240 | tf_op jit(solution)/shard_map/near/pallas_call | solution.py:529
  73.9 0.0 collective-permute-done.3.got_ref
  73.9 0.0 copy-done
  73.9 0.0 copy-done.1
  73.9 3.2 %last.1 = bf16[640,1024]{1,0:T(8,128)(2,1)} custom-call(s32[1]{0:T(128)} %bitcast.me_ref, bf16[640,1024]{1,0:T(8,128)(2,1)S(1)} %copy-done, f32[1024,512]{1,0:T(8,128)S(1)} %near.1.near_ref, f32[1024,128]{1,0:T(8,128)S(1)} %copy-done.1, bf16[1024,640]{1,0:T(8,128)(2,1)S(1)} %collective-permute-done.3.got_ref), custom_call_target="tpu_custom_call" | custom-call | flops 2621440 | bytes 6553600 | tf_op jit(solution)/shard_map/last/pallas_call | solution.py:545
Async XLA Ops:
  18.1 10.6 %collective-permute-start.2 = (bf16[1024,640]{1,0:T(8,128)(2,1)}, bf16[1024,640]{1,0:T(8,128)(2,1)S(1)}, u32[]{:S(2)}, u32[]{:S(2)}) collective-permute-start(bf16[1024,640]{1,0:T(8,128)(2,1)} %get-tuple-element.17), channel_id=1, source_target_pairs={{0,1},{1,0},{2,3},{3,2},{4,5},{5,4},{6,7},{7,6},{8,9},{9,8},{10,11... | collective-permute-start | bytes 3932168 | tf_op jit(solution)/shard_map/ppermute | solution.py:479
  18.7 10.1 %collective-permute-start = (bf16[1024,640]{1,0:T(8,128)(2,1)}, bf16[1024,640]{1,0:T(8,128)(2,1)S(1)}, u32[]{:S(2)}, u32[]{:S(2)}) collective-permute-start(bf16[1024,640]{1,0:T(8,128)(2,1)} %get-tuple-element.15.own_hbm), channel_id=1, source_target_pairs={{0,1},{1,0},{2,3},{3,2},{4,5},{5,4},{6,7},{7,6},{8,9},{9,8},{10,11... | collective-permute-start | bytes 3932168 | tf_op jit(solution)/shard_map/ppermute | solution.py:477
  18.7 10.0 %collective-permute-start.1 = (f32[1,640]{1,0:T(1,128)}, f32[1,640]{1,0:T(1,128)S(1)}, u32[]{:S(2)}, u32[]{:S(2)}) collective-permute-start(f32[1,640]{1,0:T(1,128)} %get-tuple-element.16.tv_hbm), channel_id=1, source_target_pairs={{0,1},{1,0},{2,3},{3,2},{4,5},{5,4},{6,7},{7,6},{8,9},{9,8},{10,11... | collective-permute-start | bytes 7688 | tf_op jit(solution)/shard_map/ppermute | solution.py:478
  64.6 9.3 %collective-permute-start.3 = (bf16[1024,640]{1,0:T(8,128)(2,1)}, bf16[1024,640]{1,0:T(8,128)(2,1)S(1)}, u32[]{:S(2)}, u32[]{:S(2)}) collective-permute-start(bf16[1024,640]{1,0:T(8,128)(2,1)} %get-tuple-element.24), channel_id=1, source_target_pairs={{0,1},{1,0},{2,3},{3,2},{4,5},{5,4},{6,7},{7,6},{8,9},{9,8},{10,11... | collective-permute-start | bytes 3932168 | tf_op jit(solution)/shard_map/ppermute | solution.py:527
  64.7 9.2 %copy-start = (bf16[640,1024]{1,0:T(8,128)(2,1)S(1)}, bf16[640,1024]{1,0:T(8,128)(2,1)}, u32[]{:S(2)}) copy-start(bf16[640,1024]{1,0:T(8,128)(2,1)} %x_ref.1) | copy-start | bytes 3932164
  64.7 9.2 %copy-start.1 = (f32[1024,128]{1,0:T(8,128)S(1)}, f32[1024,128]{1,0:T(8,128)}, u32[]{:S(2)}) copy-start(f32[1024,128]{1,0:T(8,128)} %get-tuple-element.23.mixed_ref) | copy-start | bytes 1572868

commit v4 on v3

--- a/solution.py
+++ b/solution.py
@@ -20,7 +20,7 @@
 F32 = jnp.float32
 WIDE = 256
 LANES = 128
-CHUNK = 2 * S
+CHUNK = 4 * S
 NORM = 8 * S
 FRONT_MIB = 32
 COVER_MIB = 24

time: 77.5 us -> 77.4 us (level)
  no operation moved by 1% of the time
where the time goes in v4:
time: 77.4 us; the launch traced here: 77 us
  Pallas kernels  75.1 us (97%)
  starting transfers between devices  1.12 us (1%)
    pallas_call x1, Pallas kernels, local_pair(): pl.pallas_call(functools.partial(stage_middle, size=size, tiles=tiles), n...  35.9 us
    pallas_call x1, Pallas kernels, local_pair(): pl.pallas_call(functools.partial(stage_front, size=size, tiles=tiles), na...  17.4 us
    pallas_call x1, Pallas kernels, local_pair(): pl.pallas_call(functools.partial(stage_cover, tiles=tiles), name='cover',...  9.54 us
    pallas_call x1, Pallas kernels, local_pair(): pl.pallas_call(functools.partial(stage_near, tiles=tiles), name='near', o...  9.15 us
    pallas_call x1, Pallas kernels, local_pair(): pl.pallas_call(stage_last, name='last', out_shape=jax.ShapeDtypeStruct((c...  3.17 us
  transfers between devices with their start and end apart: 4, of which 0 were waited for; matrix products, arithmetic and copies ran while one was open for 0% of the time, Pallas kernels for 24%

profile of v4, /device:TPU:0, one launch (start us, length us, event | category | flops | bytes accessed | tf_op | source)
XLA Modules:
  0.0 77.0 jit_solution(14336504631216267293)
XLA Ops:
  0.7 17.4 %front.1 = (bf16[1024,640]{1,0:T(8,128)(2,1)}, f32[1,640]{1,0:T(1,128)}, bf16[1024,640]{1,0:T(8,128)(2,1)}, f32[1024,128]{1,0:T(8,128)}, bf16[1024,640]{1,0:T(8,128)(2,1)}, /*index=5*/bf16[1088,1920]{1,0:T(8,128)(2,1)S(1)}) custom-call(s32[1]{0:T(128)} %bitcast.me_ref, s32[1]{0:T(128)S(6)} %copy.15.step_ref, bf16[640,1024]{1,0:T(8,128)(2,1)} %x_ref.1, ...), custom_call_target="tpu_custom_call" | custom-call | flops 9059696640 | bytes 8847360 | tf_op jit(solution)/shard_map/front/pallas_call | solution.py:452
  18.0 0.5 collective-permute-start.2
  18.6 0.1 collective-permute-start
  18.6 0.4 collective-permute-start.1
  19.1 9.5 %cover.1.near_hbm = f32[1024,512]{1,0:T(8,128)} custom-call(s32[1]{0:T(128)} %bitcast.me_ref, bf16[1088,1920]{1,0:T(8,128)(2,1)S(1)} %get-tuple-element.18.sh, bf16[9,640,1280]{2,1,0:T(8,128)(2,1)} %w_hbm.4), custom_call_target="tpu_custom_call" | custom-call | flops 6039797760 | bytes 5898240 | tf_op jit(solution)/shard_map/cover/pallas_call | solution.py:481
  28.6 0.0 collective-permute-done.1.tvgot
  28.6 0.0 collective-permute-done.2.cgot
  28.6 0.0 collective-permute-done.got_ref
  28.6 35.9 %middle.1 = (bf16[1024,640]{1,0:T(8,128)(2,1)}, f32[1024,128]{1,0:T(8,128)}, bf16[1088,1920]{1,0:T(8,128)(2,1)S(1)}, bf16[1024,640]{1,0:T(8,128)(2,1)S(1)}) custom-call(s32[1]{0:T(128)} %bitcast.me_ref, s32[8,8]{1,0:T(8,128)} %bitcast.4, bf16[1024,640]{1,0:T(8,128)(2,1)S(1)} %collective-permute-done.got_ref, f32[1,640]{1,0:T(1,128)S(1)} %collective-permute-done.1.tvgot, ...), custom_call_target="tpu_custom_call" | custom-call | flops 24159191040 | bytes 23592960 | tf_op jit(solution)/shard_map/middle/pallas_call | solution.py:497
  64.5 0.1 collective-permute-start.3
  64.6 0.0 copy-start
  64.6 0.0 copy-start.1
  64.6 9.2 %near.1.near_ref = f32[1024,512]{1,0:T(8,128)S(1)} custom-call(s32[1]{0:T(128)} %bitcast.me_ref, bf16[1088,1920]{1,0:T(8,128)(2,1)S(1)} %get-tuple-element.21.sh, bf16[1024,640]{1,0:T(8,128)(2,1)S(1)} %get-tuple-element.22.state, bf16[9,640,1280]{2,1,0:T(8,128)(2,1)} %w_hbm.5, bf16[640,1280]{1,0:T(8,128)(2,1)} %z_hbm.3), custom_call_target="tpu_custom_call" | custom-call | flops 6039797760 | bytes 5898240 | tf_op jit(solution)/shard_map/near/pallas_call | solution.py:529
  73.8 0.0 collective-permute-done.3.got_ref
  73.8 0.0 copy-done
  73.8 0.0 copy-done.1
  73.8 3.2 %last.1 = bf16[640,1024]{1,0:T(8,128)(2,1)} custom-call(s32[1]{0:T(128)} %bitcast.me_ref, bf16[640,1024]{1,0:T(8,128)(2,1)S(1)} %copy-done, f32[1024,512]{1,0:T(8,128)S(1)} %near.1.near_ref, f32[1024,128]{1,0:T(8,128)S(1)} %copy-done.1, bf16[1024,640]{1,0:T(8,128)(2,1)S(1)} %collective-permute-done.3.got_ref), custom_call_target="tpu_custom_call" | custom-call | flops 2621440 | bytes 6553600 | tf_op jit(solution)/shard_map/last/pallas_call | solution.py:545
Async XLA Ops:
  18.0 10.6 %collective-permute-start.2 = (bf16[1024,640]{1,0:T(8,128)(2,1)}, bf16[1024,640]{1,0:T(8,128)(2,1)S(1)}, u32[]{:S(2)}, u32[]{:S(2)}) collective-permute-start(bf16[1024,640]{1,0:T(8,128)(2,1)} %get-tuple-element.17), channel_id=1, source_target_pairs={{0,1},{1,0},{2,3},{3,2},{4,5},{5,4},{6,7},{7,6},{8,9},{9,8},{10,11... | collective-permute-start | bytes 3932168 | tf_op jit(solution)/shard_map/ppermute | solution.py:479
  18.6 10.1 %collective-permute-start = (bf16[1024,640]{1,0:T(8,128)(2,1)}, bf16[1024,640]{1,0:T(8,128)(2,1)S(1)}, u32[]{:S(2)}, u32[]{:S(2)}) collective-permute-start(bf16[1024,640]{1,0:T(8,128)(2,1)} %get-tuple-element.15.own_hbm), channel_id=1, source_target_pairs={{0,1},{1,0},{2,3},{3,2},{4,5},{5,4},{6,7},{7,6},{8,9},{9,8},{10,11... | collective-permute-start | bytes 3932168 | tf_op jit(solution)/shard_map/ppermute | solution.py:477
  18.6 10.0 %collective-permute-start.1 = (f32[1,640]{1,0:T(1,128)}, f32[1,640]{1,0:T(1,128)S(1)}, u32[]{:S(2)}, u32[]{:S(2)}) collective-permute-start(f32[1,640]{1,0:T(1,128)} %get-tuple-element.16.tv_hbm), channel_id=1, source_target_pairs={{0,1},{1,0},{2,3},{3,2},{4,5},{5,4},{6,7},{7,6},{8,9},{9,8},{10,11... | collective-permute-start | bytes 7688 | tf_op jit(solution)/shard_map/ppermute | solution.py:478
  64.5 9.3 %collective-permute-start.3 = (bf16[1024,640]{1,0:T(8,128)(2,1)}, bf16[1024,640]{1,0:T(8,128)(2,1)S(1)}, u32[]{:S(2)}, u32[]{:S(2)}) collective-permute-start(bf16[1024,640]{1,0:T(8,128)(2,1)} %get-tuple-element.24), channel_id=1, source_target_pairs={{0,1},{1,0},{2,3},{3,2},{4,5},{5,4},{6,7},{7,6},{8,9},{9,8},{10,11... | collective-permute-start | bytes 3932168 | tf_op jit(solution)/shard_map/ppermute | solution.py:527
  64.6 9.2 %copy-start = (bf16[640,1024]{1,0:T(8,128)(2,1)S(1)}, bf16[640,1024]{1,0:T(8,128)(2,1)}, u32[]{:S(2)}) copy-start(bf16[640,1024]{1,0:T(8,128)(2,1)} %x_ref.1) | copy-start | bytes 3932164
  64.6 9.2 %copy-start.1 = (f32[1024,128]{1,0:T(8,128)S(1)}, f32[1024,128]{1,0:T(8,128)}, u32[]{:S(2)}) copy-start(f32[1024,128]{1,0:T(8,128)} %get-tuple-element.23.mixed_ref) | copy-start | bytes 1572868
